TPU v7x, 32 devices: a whole 2x2x4 slice. The times are simulated.
32 devices in a mesh: seq: 16 (over z, y, x), head: 2 (over core).
Axes of the slice: x: 2, y: 2, z: 4, core: 2. Of those that a mesh axis runs over, the one named last changes fastest.
Arguments:
- query_elements: bfloat16 [16384, 4096], P('seq', 'head'), may hold values from -4 to 4
- query_exponents: int32 [16384, 128], P('seq', 'head'), may hold values from -1 to 1
- key_elements: bfloat16 [16384, 512], P('seq', 'head'), may hold values from -4 to 4
- key_exponents: int32 [16384, 16], P('seq', 'head'), may hold values from -1 to 1
- value_elements: bfloat16 [16384, 512], P('seq', 'head'), may hold values from -4 to 4
- value_exponents: int32 [16384, 16], P('seq', 'head'), may hold values from -1 to 1
- query_clip_words: int32 [16384, 256], P('seq', 'head'), may hold values from 0 to 65280, as said below
- key_clip_words: int32 [16384, 32], P('seq', 'head'), may hold values from 0 to 65280, as said below
- sinks: float32 [64], P('head'), may hold values from -2 to 2
- rotation: float32 [8, 64, 64], P('head'), may hold values from -0.75 to 0.75
- output_gradient: bfloat16 [16384, 4096], P('seq', 'head'), may hold values from -120 to 120
Outputs:
- grad_q: bfloat16 [16384, 4096], P('seq', 'head')
- key_gradient_raw: bfloat16 [16384, 512], P('seq', 'head')
- value_gradient: bfloat16 [16384, 512], P('seq', 'head')
- grad_rotation: float32 [8, 64, 64], P('head')
- grad_sinks: float32 [64], P('head')
Inputs may be any that keep to these rules, and one draw needn't show every extreme that they name: `query_clip_words`: bit b of word w of a row is 1 where entry 16 w + b of the row passed the clip; a word whose upper eight bits are all set has its lower eight bits clear. `key_clip_words`: bit b of word w of a row is 1 where entry 16 w + b of the row passed the clip; a word whose upper eight bits are all set has its lower eight bits clear.
All inputs are finite; a program needn't handle non-finite values.
Results may differ from a plain program's by a relative error of at most 0.0097.
Values may be sent and summed in bfloat16 or wider, within the bound.
No kernel may reach another device: no remote copies, remote signals or barrier semaphores. Data moves between devices by JAX's collectives and lax.ppermute only.
A program may use at most 128 MiB of HBM per device.

v0:
```python
import math

import jax
import jax.numpy as jnp
from jax import lax
from jax.sharding import PartitionSpec as P

WINDOW = 128
SHARED_EXPONENT = 32


clip_scale = 64.0
limit_factor = 0.05
negative = -1e30


def from_behind(block, axis, distance):
    devices = range(lax.axis_size(axis))
    route = [(i - distance, i) for i in devices if i - distance in devices]
    return lax.ppermute(block, axis, route)


def decode_blocks(element_vals, powers):
    row_count = element_vals.shape[0]
    scaled = (
        element_vals.astype(jnp.float32).reshape(row_count, -1, SHARED_EXPONENT)
        * jnp.exp2(powers.astype(jnp.float32))[:, :, None]
    )
    return scaled.reshape(row_count, -1).astype(jnp.bfloat16)


def unpack_words(packed):
    shifts = jnp.arange(16, dtype=jnp.int32)
    bit_vals = jnp.right_shift(packed[:, :, None], shifts[None, None, :]) & 1
    return bit_vals.reshape(packed.shape[0], -1).astype(jnp.float32)


def attend(query_blk, dout_blk, keys_blk, values, sink_logit, query_pos, key_pos):
    temper = query_blk.shape[-1] ** (-0.5)
    scores = (
        jnp.einsum("igqd,jgd->gqij", query_blk, keys_blk, preferred_element_type=jnp.float32)
        * temper
    )
    allowed = (
        (key_pos[None, :] <= query_pos[:, None])
        & (key_pos[None, :] > query_pos[:, None] - WINDOW)
        & (key_pos[None, :] >= 0)
    )
    scores = jnp.where(allowed, scores, negative)
    row_max = jnp.maximum(jnp.max(scores, axis=3), sink_logit[:, :, None])
    numerators = jnp.where(allowed, jnp.exp(scores - row_max[..., None]), 0.0)
    totals = jnp.sum(numerators, axis=3) + jnp.exp(sink_logit[:, :, None] - row_max)
    weights = numerators / totals[..., None]
    rounded = weights.astype(jnp.bfloat16)
    outputs = jnp.einsum("gqij,jgd->igqd", rounded, values, preferred_element_type=jnp.float32)
    deltas = jnp.transpose(jnp.sum(dout_blk.astype(jnp.float32) * outputs, axis=3), (1, 2, 0))
    grad_probs = jnp.einsum("igqd,jgd->gqij", dout_blk, values, preferred_element_type=jnp.float32)
    grad_scores = (weights * (grad_probs - deltas[..., None])).astype(jnp.bfloat16)
    grad_query = (
        jnp.einsum("gqij,jgd->igqd", grad_scores, keys_blk, preferred_element_type=jnp.float32)
        * temper
    )
    grad_keys = (
        jnp.einsum("gqij,igqd->jgd", grad_scores, query_blk, preferred_element_type=jnp.float32)
        * temper
    )
    grad_vals = jnp.einsum("gqij,igqd->jgd", rounded, dout_blk, preferred_element_type=jnp.float32)
    sink_terms = -jnp.sum(jnp.exp(sink_logit[:, :, None] - row_max) / totals * deltas, axis=2)
    return (grad_query, grad_keys, grad_vals, sink_terms, (row_max, totals, deltas))


def rim_terms(query_blk, dout_blk, row_max, totals, deltas, keys_blk, values):
    temper = query_blk.shape[-1] ** (-0.5)
    scores = (
        jnp.einsum("igqd,jgd->gqij", query_blk, keys_blk, preferred_element_type=jnp.float32)
        * temper
    )
    positions = jnp.arange(WINDOW, dtype=jnp.int32)
    allowed = positions[None, :] > positions[:, None]
    numerators = jnp.where(allowed, jnp.exp(scores - row_max[..., None]), 0.0)
    weights = numerators / jnp.maximum(totals, 1.0)[..., None]
    rounded = weights.astype(jnp.bfloat16)
    grad_probs = jnp.einsum("igqd,jgd->gqij", dout_blk, values, preferred_element_type=jnp.float32)
    grad_scores = (weights * (grad_probs - deltas[..., None])).astype(jnp.bfloat16)
    grad_keys = (
        jnp.einsum("gqij,igqd->jgd", grad_scores, query_blk, preferred_element_type=jnp.float32)
        * temper
    )
    grad_vals = jnp.einsum("gqij,igqd->jgd", rounded, dout_blk, preferred_element_type=jnp.float32)
    return (grad_keys, grad_vals)


def run_blocks(query_rows_list, douts, key_ext, value_ext, offset, sink_logit):
    block_count = query_rows_list.shape[0] // WINDOW

    def block(block_index):
        begin_row = block_index * WINDOW
        query_b = lax.dynamic_slice_in_dim(query_rows_list, begin_row, WINDOW, 0)
        dout_b = lax.dynamic_slice_in_dim(douts, begin_row, WINDOW, 0)
        keys_b = lax.dynamic_slice_in_dim(key_ext, begin_row, 2 * WINDOW, 0)
        values_b = lax.dynamic_slice_in_dim(value_ext, begin_row, 2 * WINDOW, 0)
        query_pos = offset + begin_row + jnp.arange(WINDOW, dtype=jnp.int32)
        key_pos = offset + begin_row - WINDOW + jnp.arange(2 * WINDOW, dtype=jnp.int32)
        return attend(query_b, dout_b, keys_b, values_b, sink_logit, query_pos, key_pos)

    return lax.map(block, jnp.arange(block_count, dtype=jnp.int32))


def per_device(
    query_elements,
    query_exponents,
    key_elements,
    key_exponents,
    value_elements,
    value_exponents,
    query_clip_words,
    key_clip_words,
    sinks,
    rotation,
    output_gradient,
):
    row_count = query_elements.shape[0]
    local_groups = rotation.shape[0]
    head_dim = rotation.shape[1]
    per_group = sinks.shape[0] // local_groups
    query_rows_list = decode_blocks(query_elements, query_exponents).reshape(
        row_count, local_groups, per_group, head_dim
    )
    key_row_list = decode_blocks(key_elements, key_exponents).reshape(
        row_count, local_groups, head_dim
    )
    value_row_list = decode_blocks(value_elements, value_exponents).reshape(
        row_count, local_groups, head_dim
    )
    output_grad_list = output_gradient.reshape(row_count, local_groups, per_group, head_dim)
    sink_row_list = sinks.reshape(local_groups, per_group)
    offset = lax.axis_index("seq") * row_count
    all_tokens = row_count * lax.axis_size("seq")
    all_heads = sinks.shape[0] * lax.axis_size("head")
    limit_value = limit_factor * math.sqrt(all_tokens * all_heads * head_dim)
    inner = run_blocks(
        query_rows_list[WINDOW:],
        output_grad_list[WINDOW:],
        key_row_list,
        value_row_list,
        offset + WINDOW,
        sink_row_list,
    )
    prev_keys, prev_vals = from_behind(
        (key_row_list[row_count - WINDOW :], value_row_list[row_count - WINDOW :]), "seq", 1
    )
    first_block = run_blocks(
        query_rows_list[:WINDOW],
        output_grad_list[:WINDOW],
        jnp.concatenate([prev_keys, key_row_list[:WINDOW]], 0),
        jnp.concatenate([prev_vals, value_row_list[:WINDOW]], 0),
        offset,
        sink_row_list,
    )
    results = jax.tree.map(
        lambda first_part, second_part: jnp.concatenate([first_part, second_part], 0),
        first_block,
        inner,
    )
    grad_query, grad_keys, grad_vals, sink_terms, row_stats = results
    next_query, next_dout = from_behind(
        (query_rows_list[:WINDOW], output_grad_list[:WINDOW]), "seq", -1
    )
    next_max, next_total, next_delta = from_behind(
        (row_stats[0][0], row_stats[1][0], row_stats[2][0]), "seq", -1
    )
    back_keys, back_vals = rim_terms(
        next_query,
        next_dout,
        next_max,
        next_total,
        next_delta,
        key_row_list[row_count - WINDOW :],
        value_row_list[row_count - WINDOW :],
    )
    key_total = grad_keys[:, WINDOW:] + jnp.concatenate(
        [grad_keys[1:, :WINDOW], back_keys[None]], 0
    )
    value_total = grad_vals[:, WINDOW:] + jnp.concatenate(
        [grad_vals[1:, :WINDOW], back_vals[None]], 0
    )
    key_total = key_total.reshape(row_count, local_groups, head_dim)
    value_gradient = value_total.reshape(row_count, local_groups * head_dim).astype(jnp.bfloat16)
    grad_query = grad_query.reshape(row_count, local_groups, per_group, head_dim)
    query_flags = unpack_words(query_clip_words).reshape(
        row_count, local_groups, per_group, head_dim
    )
    key_flags = unpack_words(key_clip_words).reshape(row_count, local_groups, head_dim)
    masked_query = (grad_query * query_flags).astype(jnp.bfloat16)
    masked_keys = (key_total * key_flags).astype(jnp.bfloat16)
    rotation_low = rotation.astype(jnp.bfloat16)
    grad_q = jnp.einsum(
        "tgqd,ged->tgqe", masked_query, rotation_low, preferred_element_type=jnp.float32
    )
    grad_q = grad_q.astype(jnp.bfloat16).reshape(row_count, -1)
    key_gradient_raw = jnp.einsum(
        "tgd,ged->tge", masked_keys, rotation_low, preferred_element_type=jnp.float32
    )
    key_gradient_raw = key_gradient_raw.astype(jnp.bfloat16).reshape(row_count, -1)
    partial_value = jnp.einsum(
        "tgqd,tgqe->gde", query_rows_list, masked_query, preferred_element_type=jnp.float32
    )
    partial_value = partial_value + jnp.einsum(
        "tgd,tge->gde", key_row_list, masked_keys, preferred_element_type=jnp.float32
    )
    sink_part = jnp.sum(sink_terms, axis=0).reshape(-1)
    summed, sink_sum = lax.psum((partial_value, sink_part), "seq")
    raw_grad = jnp.einsum("gde,gef->gdf", rotation, summed, precision=lax.Precision.HIGHEST)
    squares = lax.psum(jnp.sum(raw_grad * raw_grad), "head")
    grad_rotation = raw_grad * (clip_scale / jnp.maximum(jnp.sqrt(squares), limit_value))
    return (grad_q, key_gradient_raw, value_gradient, grad_rotation, sink_sum)


def solution(mesh):
    return jax.shard_map(
        per_device,
        mesh=mesh,
        in_specs=(
            P("seq", "head"),
            P("seq", "head"),
            P("seq", "head"),
            P("seq", "head"),
            P("seq", "head"),
            P("seq", "head"),
            P("seq", "head"),
            P("seq", "head"),
            P("head"),
            P("head", None, None),
            P("seq", "head"),
        ),
        out_specs=(
            P("seq", "head"),
            P("seq", "head"),
            P("seq", "head"),
            P("head", None, None),
            P("head"),
        ),
        check_vma=False,
    )
```

profile of v0, /device:TPU:0, one launch (start us, length us, event | category | flops | bytes accessed | tf_op | source)
XLA Modules:
  0.0 384.2 jit_solution(17470363671863529029)
XLA Ops:
  10.1 4.9 %collective-permute-start = (bf16[128,4,64]{0,2,1:T(8,128)(2,1)}, bf16[128,4,64]{0,2,1:T(8,128)(2,1)S(1)}, u32[]{:S(2)}, u32[]{:S(2)}) collective-permute-start(bf16[128,4,64]{0,2,1:T(8,128)(2,1)} %bitcast.23), channel_id=1, source_target_pairs={{0,2},{2,4},{4,6},{6,8},{8,10},{10,12},{12,14},{14,16},{16,18},{18... | collective-permute-start | bytes 196616 | tf_op jit(solution)/shard_map/ppermute | solution.py:20
  18.6 4.0 %collective-permute-start.1 = (bf16[128,4,64]{0,2,1:T(8,128)(2,1)}, bf16[128,4,64]{0,2,1:T(8,128)(2,1)}, u32[]{:S(2)}, u32[]{:S(2)}) collective-permute-start(bf16[128,4,64]{0,2,1:T(8,128)(2,1)} %bitcast.32), channel_id=1, source_target_pairs={{0,2},{2,4},{4,6},{6,8},{8,10},{10,12},{12,14},{14,16},{16,18},{18... | collective-permute-start | bytes 196616 | tf_op jit(solution)/shard_map/ppermute | solution.py:20
  24.9 6.4 %copy.49 = bf16[1024,2048]{0,1:T(8,128)(2,1)} copy(bf16[1024,2048]{1,0:T(8,128)(2,1)} %param.13) | data formatting | bytes 8388608 | tf_op args[0]
  31.3 3.4 fusion.38
  40.9 4.5 %slice.78 = bf16[896,2048]{1,0:T(8,128)(2,1)} slice(bf16[1024,2048]{1,0:T(8,128)(2,1)} %param.23), slice={[128:1024], [0:2048]} | slice | bytes 7340032 | tf_op jit(solution)/shard_map/slice | solution.py:143
  45.4 2.4 slice.89
  49.4 6.1 %copy.54 = bf16[896,2048]{0,1:T(8,128)(2,1)} copy(bf16[896,2048]{1,0:T(8,128)(2,1)} %slice.78) | data formatting | bytes 7340032 | tf_op jit(solution)/shard_map/slice | solution.py:143
  55.5 114.1 %while.14 = (s32[]{:T(128)}, f32[7,128,4,8,64]{1,4,3,2,0:T(8,128)}, f32[7,256,4,64]{1,3,2,0:T(8,128)}, f32[7,256,4,64]{1,3,2,0:T(8,128)S(1)}, f32[7,4,8]{2,1,0:T...) while((s32[]{:T(128)}, f32[7,128,4,8,64]{1,4,3,2,0:T(8,128)}, ...), condition=%wide.region_8.9_spmd, body=%wide.region_3.8_spmd.sunk | while | flops 835941376 | bytes 34596468 | solution.py:106
  60.3 2.4 fusion.146
  62.9 2.3 fusion.150
  65.2 2.7 fusion.147
  67.9 2.5 fusion.149
  76.6 2.4 fusion.146
  79.2 2.3 fusion.150
  81.5 2.7 fusion.147
  84.1 2.5 fusion.149
  92.9 2.4 fusion.146
  95.5 2.3 fusion.150
  97.8 2.7 fusion.147
  100.5 2.5 fusion.149
  109.2 2.4 fusion.146
  111.8 2.3 fusion.150
  114.1 2.7 fusion.147
  116.7 2.5 fusion.149
  125.5 2.4 fusion.146
  128.1 2.3 fusion.150
  130.4 2.7 fusion.147
  133.1 2.5 fusion.149
  141.8 2.4 fusion.146
  144.4 2.3 fusion.150
  146.7 2.7 fusion.147
  149.3 2.5 fusion.149
  158.1 2.4 fusion.146
  160.7 2.3 fusion.150
  163.0 2.7 fusion.147
  165.7 2.5 fusion.149
  179.2 3.0 convolution_bitcast_fusion.4
  182.2 2.5 fusion.51
  186.0 2.7 fusion.40
  188.7 2.7 fusion.53
  197.8 3.2 convolution_convert_fusion
  201.2 6.4 %copy.63 = bf16[1024,2048]{1,0:T(8,128)(2,1)} copy(bf16[1024,2048]{0,1:T(8,128)(2,1)} %bitcast.325) | data formatting | bytes 8388608
  207.7 50.7 %psum.23 = f32[32]{0:T(128)} all-reduce(f32[32]{0:T(128)S(1)} %reduce_sum.105), channel_id=1, replica_groups=mesh['seq'=16,'head'=2] {'seq'}, use_global_device_ids=true, to_apply=%region_14.15 | all-reduce | flops 32 | bytes 256 | tf_op jit(solution)/shard_map/psum | solution.py:212
  258.3 2.9 fusion.91
  261.3 3.1 fusion.55
  269.5 2.5 convolution_bitcast_fusion.7
  274.4 96.5 %all-reduce.2.cloned.1.call-done = f32[4,64,64]{1,2,0:T(8,128)} async-done(((f32[4,64,64]{1,2,0:T(8,128)}), f32[4,64,64]{1,2,0:T(8,128)}) %all-reduce.2.cloned.1.call-update) | async-done | bytes 65552 | tf_op jit(solution)/shard_map/psum | solution.py:212
  372.7 3.1 psum.22
  (229 shorter events, 83.5 us)
Async XLA Ops:
  7.2 15.4 %slice-start.2 = ((bf16[1024,2048]{1,0:T(8,128)(2,1)}), bf16[128,2048]{1,0:T(8,128)(2,1)S(1)}, s32[]{:S(2)}) async-start(bf16[1024,2048]{1,0:T(8,128)(2,1)} %param.23), calls=%async_computation.3 | async-start | bytes 1048576 | tf_op jit(solution)/shard_map/slice | solution.py:154
  7.2 17.7 %copy-start.10 = (s32[1024,64]{0,1:T(8,128)S(1)}, s32[1024,64]{0,1:T(8,128)}, u32[]{:S(2)}) copy-start(s32[1024,64]{0,1:T(8,128)} %param.14) | copy-start | bytes 786436
  7.2 363.7 %all-reduce.2.cloned.1.call-start = ((), (), s32[]{:S(2)}) async-start(), calls=%async_computation | async-start | bytes 262144 | tf_op jit(solution)/shard_map/psum | solution.py:212
  10.1 163.1 %collective-permute-start = (bf16[128,4,64]{0,2,1:T(8,128)(2,1)}, bf16[128,4,64]{0,2,1:T(8,128)(2,1)S(1)}, u32[]{:S(2)}, u32[]{:S(2)}) collective-permute-start(bf16[128,4,64]{0,2,1:T(8,128)(2,1)} %bitcast.23), channel_id=1, source_target_pairs={{0,2},{2,4},{4,6},{6,8},{8,10},{10,12},{12,14},{14,16},{16,18},{18... | collective-permute-start | bytes 196616 | tf_op jit(solution)/shard_map/ppermute | solution.py:20
  17.1 0.8 copy-start.6
  18.6 163.6 %collective-permute-start.1 = (bf16[128,4,64]{0,2,1:T(8,128)(2,1)}, bf16[128,4,64]{0,2,1:T(8,128)(2,1)}, u32[]{:S(2)}, u32[]{:S(2)}) collective-permute-start(bf16[128,4,64]{0,2,1:T(8,128)(2,1)} %bitcast.32), channel_id=1, source_target_pairs={{0,2},{2,4},{4,6},{6,8},{8,10},{10,12},{12,14},{14,16},{16,18},{18... | collective-permute-start | bytes 196616 | tf_op jit(solution)/shard_map/ppermute | solution.py:20
  23.6 237.6 %collective-permute-start.5 = (bf16[128,4,8,64]{0,3,2,1:T(8,128)(2,1)}, bf16[128,4,8,64]{0,3,2,1:T(8,128)(2,1)}, u32[]{:S(2)}, u32[]{:S(2)}) collective-permute-start(bf16[128,4,8,64]{0,3,2,1:T(8,128)(2,1)} %bitcast.36), channel_id=1, source_target_pairs={{2,0},{4,2},{6,4},{8,6},{10,8},{12,10},{14,12},{16,14},{18,16},{20... | collective-permute-start | bytes 1572872 | tf_op jit(solution)/shard_map/ppermute | solution.py:20
  34.7 2.0 copy-start
  37.7 220.6 %collective-permute-start.2 = (bf16[128,4,8,64]{0,3,2,1:T(8,128)(2,1)}, bf16[128,4,8,64]{0,3,2,1:T(8,128)(2,1)}, u32[]{:S(2)}, u32[]{:S(2)}) collective-permute-start(bf16[128,4,8,64]{0,3,2,1:T(8,128)(2,1)} %bitcast.29), channel_id=1, source_target_pairs={{2,0},{4,2},{6,4},{8,6},{10,8},{12,10},{14,12},{16,14},{18,16},{20... | collective-permute-start | bytes 1572872 | tf_op jit(solution)/shard_map/ppermute | solution.py:20
  40.9 4.5 %copy-start.1 = (bf16[1024,2048]{0,1:T(8,128)(2,1)S(1)}, bf16[1024,2048]{0,1:T(8,128)(2,1)}, u32[]{:S(2)}) copy-start(bf16[1024,2048]{0,1:T(8,128)(2,1)} %copy-done) | copy-start | bytes 12582916
  45.4 2.4 copy-start.14
  45.4 3.8 copy-start.8
  49.4 6.1 %copy-start.15 = (f32[32]{0:T(128)S(1)}, f32[32]{0:T(128)}, u32[]{:S(2)}) copy-start(f32[32]{0:T(128)} %param.21) | copy-start | bytes 388
  49.4 6.1 %copy-start.19 = (f32[7,4,8]{2,1,0:T(4,128)S(1)}, f32[7,4,8]{2,1,0:T(4,128)}, u32[]{:S(2)}) copy-start(f32[7,4,8]{2,1,0:T(4,128)} %custom-call.3) | copy-start | bytes 2692
  55.5 117.5 %copy-start.21 = (s32[256]{0:T(256)S(1)}, s32[256]{0:T(256)}, u32[]{:S(2)}) copy-start(s32[256]{0:T(256)} %iota_add_fusion.2) | copy-start | bytes 3076
  55.5 117.5 %copy-start.22 = (pred[256]{0:T(512)(128)(4,1)S(1)}, pred[256]{0:T(512)(128)(4,1)}, u32[]{:S(2)}) copy-start(pred[256]{0:T(512)(128)(4,1)} %broadcast_compare_fusion.1) | copy-start | bytes 772
  55.5 117.5 %copy-start.23 = (s32[128]{0:T(128)S(1)}, s32[128]{0:T(128)}, u32[]{:S(2)}) copy-start(s32[128]{0:T(128)} %get-tuple-element.345) | copy-start | bytes 1540
  55.5 117.5 %copy-start.24 = (s32[128]{0:T(128)S(1)}, s32[128]{0:T(128)}, u32[]{:S(2)}) copy-start(s32[128]{0:T(128)} %get-tuple-element.346) | copy-start | bytes 1540
  57.2 3.1 copy-start.7
  73.4 3.1 copy-start.7
  89.8 3.1 copy-start.7
  106.0 3.1 copy-start.7
  122.4 3.1 copy-start.7
  138.6 3.1 copy-start.7
  155.0 3.1 copy-start.7
  169.6 5.4 %copy-start.13 = (f32[4,8]{1,0:T(4,128)S(1)}, f32[4,8]{1,0:T(4,128)}, u32[]{:S(2)}) copy-start(f32[4,8]{1,0:T(4,128)} %max.75) | copy-start | bytes 388
  173.2 88.1 %copy-start.16 = (pred[128,128]{0,1:T(8,128)(4,1)}, pred[128,128]{0,1:T(8,128)(4,1)S(1)}, u32[]{:S(2)}) copy-start(pred[128,128]{0,1:T(8,128)(4,1)S(1)} %iota_compare_fusion) | copy-start | bytes 49156
  175.1 86.1 %collective-permute-start.3 = (f32[4,8,128]{2,1,0:T(8,128)S(1)}, f32[4,8,128]{2,1,0:T(8,128)S(1)}, u32[]{:S(2)}, u32[]{:S(2)}) collective-permute-start(f32[4,8,128]{2,1,0:T(8,128)S(1)} %broadcast_maximum_fusion.2), channel_id=1, source_target_pairs={{2,0},{4,2},{6,4},{8,6},{10,8},{12,10},{14,12},{16,14},{18,16},{20... | collective-permute-start | bytes 49160 | tf_op jit(solution)/shard_map/ppermute | solution.py:20
  177.5 4.7 %copy-start.12 = (bf16[128,256]{0,1:T(8,128)(2,1)S(1)}, bf16[128,256]{0,1:T(8,128)(2,1)}, u32[]{:S(2)}) copy-start(bf16[128,256]{0,1:T(8,128)(2,1)} %get-tuple-element.340) | copy-start | bytes 196612
  177.5 80.8 %collective-permute-start.4 = (f32[4,8,128]{2,1,0:T(8,128)S(1)}, f32[4,8,128]{2,1,0:T(8,128)S(1)}, u32[]{:S(2)}, u32[]{:S(2)}) collective-permute-start(f32[4,8,128]{2,1,0:T(8,128)S(1)} %fusion.78), channel_id=1, source_target_pairs={{2,0},{4,2},{6,4},{8,6},{10,8},{12,10},{14,12},{16,14},{18,16},{20... | collective-permute-start | bytes 49160 | tf_op jit(solution)/shard_map/ppermute | solution.py:20
  184.7 76.6 %collective-permute-start.6 = (f32[4,8,128]{2,1,0:T(8,128)S(1)}, f32[4,8,128]{2,1,0:T(8,128)S(1)}, u32[]{:S(2)}, u32[]{:S(2)}) collective-permute-start(f32[4,8,128]{2,1,0:T(8,128)S(1)} %bitcast.339), channel_id=1, source_target_pairs={{2,0},{4,2},{6,4},{8,6},{10,8},{12,10},{14,12},{16,14},{18,16},{20... | collective-permute-start | bytes 49160 | tf_op jit(solution)/shard_map/ppermute | solution.py:20
  188.7 4.2 %slice-start = ((s8[7340032]{0:T(1024)(128)(4,1)}), s8[4194304]{0:T(1024)(128)(4,1)S(1)}, s32[]{:S(2)}) async-start(s8[7340032]{0:T(1024)(128)(4,1)} %bitcast.328), calls=%async_computation.1 | async-start | bytes 8388608
  191.8 1.9 slice-start.1
  193.7 2.2 copy-start.2
  195.9 1.9 copy-start.4
  258.3 6.0 %copy-start.18 = (f32[4,8,128]{2,1,0:T(8,128)}, f32[4,8,128]{2,1,0:T(8,128)S(1)}, u32[]{:S(2)}) copy-start(f32[4,8,128]{2,1,0:T(8,128)S(1)} %broadcast_maximum_fusion.1) | copy-start | bytes 49156
  261.2 3.1 copy-start.25
  261.3 3.1 copy-start.11
  261.3 3.2 copy-start.5
  261.3 3.2 copy-start.20
  264.5 4.9 %copy-start.17 = (pred[128,128]{0,1:T(8,128)(4,1)S(1)}, pred[128,128]{0,1:T(8,128)(4,1)}, u32[]{:S(2)}) copy-start(pred[128,128]{0,1:T(8,128)(4,1)} %copy-done.16) | copy-start | bytes 49156
  269.5 2.5 copy-start.3
  269.5 2.5 copy-start.9
Sparse Core Ops, SparseCore 0:
  269.6 101.2 all-reduce.1
where the time goes:
time: 387 us; the launch traced here: 384 us
  matrix products  123 us (32%)
  waiting for transfers between devices  96.5 us (25%)
  blocking collectives  53.7 us (14%)
  local copies, waits for them, and re-layouts  51.3 us (13%)
  other arithmetic  22.9 us (6%)
  starting transfers between devices  15.9 us (4%)
  between operations  15.3 us (4%)
  loops' own time  5.49 us (1%)
    psum x1, waiting for transfers between devices, per_device(): summed, sink_sum = lax.psum((partial_value, sink_part), 'seq')  96.5 us
    psum x1, blocking collectives, per_device(): summed, sink_sum = lax.psum((partial_value, sink_part), 'seq')  50.7 us
    unnamed x63, local copies, waits for them, and re-layouts  23.9 us
    dot_general x8, matrix products, attend(): jnp.einsum('igqd,jgd->gqij', dout_blk, values, preferred_element_type=jnp...  21.3 us
    dot_general x8, matrix products, attend(): jnp.einsum('gqij,igqd->jgd', grad_scores, query_blk, preferred_element_ty...  20.2 us
    dot_general x8, matrix products, attend(): jnp.einsum('gqij,jgd->igqd', rounded, values, preferred_element_type=jnp....  19.3 us
    dot_general x8, matrix products, attend(): jnp.einsum('gqij,igqd->jgd', rounded, dout_blk, preferred_element_type=jn...  19.1 us
    ppermute x7, starting transfers between devices, from_behind(): return lax.ppermute(block, axis, route)  15.8 us
  transfers between devices with their start and end apart: 8, of which 1 were waited for; matrix products, arithmetic and copies ran while one was open for 47% of the time, Pallas kernels for 0%

commit v1 on v0

v1 whole, which is shorter than its diff:
```python
import functools
import math

import jax
import jax.numpy as jnp
from jax import lax
from jax.experimental import pallas as pl
from jax.experimental.pallas import tpu as pltpu
from jax.sharding import PartitionSpec as P

WINDOW = 128
SHARED_EXPONENT = 32
WORD_BITS = 16
LANES = 128
ROWS = 64
BAND = WINDOW + ROWS

clip_scale = 64.0
limit_factor = 0.05
negative = -1e30

f32 = jnp.float32
bf16 = jnp.bfloat16
i32 = jnp.int32


def iota(shape, dim):
    return lax.broadcasted_iota(i32, shape, dim)


def mm(a, b):
    return lax.dot_general(a, b, (((1,), (0,)), ((), ())), preferred_element_type=f32)


def mm_nt(a, b):
    return lax.dot_general(a, b, (((1,), (1,)), ((), ())), preferred_element_type=f32)


def mm_tn(a, b):
    return lax.dot_general(a, b, (((0,), (0,)), ((), ())), preferred_element_type=f32)


def decoded(elements, powers):
    width = elements.shape[1]
    shape = (powers.shape[1], width)
    spread = (iota(shape, 1) // SHARED_EXPONENT == iota(shape, 0)).astype(f32).astype(bf16)
    scale = mm(jnp.exp2(powers.astype(f32)).astype(bf16), spread)
    return elements * scale.astype(bf16)


def word_bytes(words):
    count = words.shape[1]
    shape = (count, LANES)
    low = (iota(shape, 1) == iota(shape, 0)).astype(f32).astype(bf16)
    high = (iota(shape, 1) == iota(shape, 0) + count).astype(f32).astype(bf16)
    first = (words & 255).astype(f32).astype(bf16)
    second = ((words >> 8) & 255).astype(f32).astype(bf16)
    return (mm(first, low) + mm(second, high)).astype(bf16)


def byte_flags(byte_rows, width):
    count = width // WORD_BITS
    shape = (LANES, width)
    lane, row = iota(shape, 1), iota(shape, 0)
    word = lane // WORD_BITS
    upper = (lane % WORD_BITS) // 8
    spread = (row == word + upper * count).astype(f32).astype(bf16)
    value = mm(byte_rows, spread).astype(i32)
    bit = jnp.left_shift(jnp.ones(value.shape, i32), iota(value.shape, 1) % 8)
    return (value & bit) != 0


def halo_kernel(k_ref, ke_ref, v_ref, ve_ref, w_ref, out_ref):
    width = k_ref.shape[1]
    out_ref[:, :width] = decoded(k_ref[...], ke_ref[...])
    out_ref[:, width : 2 * width] = decoded(v_ref[...], ve_ref[...])
    out_ref[:, 2 * width :] = word_bytes(w_ref[...])


def main_kernel(
    groups,
    per_group,
    sink_ref,
    q_ref,
    qe_ref,
    do_ref,
    qw_ref,
    k_ref,
    ke_ref,
    v_ref,
    ve_ref,
    kw_ref,
    halo_ref,
    rot_ref,
    gq_ref,
    pay_ref,
    ret_ref,
    dk_ref,
    dv_ref,
    kn,
    kz,
    vz,
    acck,
    accv,
    accp,
    accs,
    sinks,
    lowmask,
):
    b = pl.program_id(0)
    last = pl.num_programs(0) - 1
    width = k_ref.shape[1]
    pairs = width // LANES
    side = per_group // 2
    lanes = side * ROWS
    head = LANES // 2
    first_device = lax.axis_index("seq") == 0

    @pl.when(b == 0)
    def _():
        eighth = jnp.asarray(head**-0.5, bf16)
        kn[:WINDOW] = halo_ref[:, :width] * eighth
        kn[WINDOW:] = decoded(k_ref[...], ke_ref[...]) * eighth
        vals = decoded(v_ref[...], ve_ref[...])
        lane = iota((1, LANES), 1)
        for g in range(groups):
            keep = ((lane // head) == g % 2).astype(f32).astype(bf16)
            at = (g // 2) * LANES
            kz[g] = kn[:, at : at + LANES] * keep
            vz[g, :WINDOW] = halo_ref[:, width + at : width + at + LANES] * keep
            vz[g, WINDOW:] = vals[:, at : at + LANES] * keep
        acck[...] = jnp.zeros_like(acck)
        accv[...] = jnp.zeros_like(accv)
        accp[...] = jnp.zeros_like(accp)
        accs[...] = jnp.zeros_like(accs)
        pairof = iota((1, lanes), 1) // ROWS
        for g in range(groups):
            for odd in range(2):
                row = jnp.zeros((1, lanes), f32)
                for p in range(side):
                    row = jnp.where(pairof == p, sink_ref[g * per_group + 2 * p + odd], row)
                sinks[pl.ds(2 * g + odd, 1), :] = row
        lowmask[...] = (
            (iota((ROWS, lanes), 0) > iota((ROWS, lanes), 1) % ROWS).astype(f32).astype(bf16)
        )

    def body(edge):
        start = pl.multiple_of(b * ROWS, ROWS)
        q = decoded(q_ref[...], qe_ref[...])
        do = do_ref[...]
        words = jnp.transpose(qw_ref[...])
        current = iota((ROWS, lanes), 0) <= iota((ROWS, lanes), 1) % ROWS
        lower = iota((1, LANES), 1) < head
        low = lowmask[...]
        bit = jnp.left_shift(jnp.ones((head, 1), i32), iota((head, 1), 0) % WORD_BITS)
        limit = jnp.where(first_device, WINDOW, 0) - start

        def tiles(rows, g):
            return jnp.concatenate(
                [rows[:, (side * g + p) * LANES : (side * g + p + 1) * LANES] for p in range(side)],
                axis=0,
            )

        def combined(x):
            low_part, mid, high = x[:ROWS], x[ROWS : 2 * ROWS], x[2 * ROWS :]
            return jnp.concatenate([jnp.where(current, high, low_part), mid], axis=0)

        def spread(x):
            first = x[:ROWS] * low
            return jnp.concatenate([first, x[ROWS:], x[:ROWS] - first], axis=0)

        for pair in range(pairs):
            at = pair * LANES
            ktr = jnp.transpose(kn[pl.ds(start, BAND), at : at + LANES])
            sums_k, sums_v, sums_p = [], [], []
            for half in range(2):
                g = 2 * pair + half
                if g >= groups:
                    continue
                kb = kz[g, pl.ds(start, BAND), :]
                vb = vz[g, pl.ds(start, BAND), :]
                aq, ad = tiles(q, g), tiles(do, g)
                bq, bd = pltpu.roll(aq, head, 1), pltpu.roll(ad, head, 1)
                wq, wd = ([aq, bq], [ad, bd]) if half == 0 else ([bq, aq], [bd, ad])
                probs, grads, dqs = [], [], []
                for odd in range(2):
                    scores = mm_nt(kb, wq[odd])
                    if edge:
                        scores = jnp.where(iota((BAND, 1), 0) >= limit, scores, negative)
                    scores = combined(scores)
                    sink = sinks[pl.ds(2 * g + odd, 1), :]
                    row_max = jnp.maximum(jnp.max(scores, axis=0, keepdims=True), sink)
                    numer = jnp.exp(scores - row_max)
                    sink_numer = jnp.exp(sink - row_max)
                    inverse = 1.0 / (jnp.sum(numer, axis=0, keepdims=True) + sink_numer)
                    weights = numer * inverse
                    gprobs = combined(mm_nt(vb, wd[odd]))
                    delta = jnp.sum(weights * gprobs, axis=0, keepdims=True)
                    gscores = (weights * (gprobs - delta)).astype(bf16)
                    accs[pl.ds(2 * g + odd, 1), :] -= sink_numer * inverse * delta
                    probs.append(spread(weights.astype(bf16)))
                    gs = spread(gscores)
                    grads.append(gs)
                    dqs.append(mm(ktr[half * head : (half + 1) * head], gs))
                probs = jnp.concatenate(probs, axis=1)
                grads = jnp.concatenate(grads, axis=1)
                wq = jnp.concatenate(wq, axis=0)
                wd = jnp.concatenate(wd, axis=0)
                sums_k.append(mm(grads, wq))
                sums_v.append(mm(probs, wd))
                per_pair = 2 * head // WORD_BITS
                base = g * side * per_pair
                wcat = jnp.concatenate(
                    [words[base + p * per_pair : base + (p + 1) * per_pair] for p in range(side)],
                    axis=1,
                )
                masked = []
                for odd in range(2):
                    spots = jnp.concatenate(
                        [
                            jnp.broadcast_to(wcat[n : n + 1], (WORD_BITS, lanes))
                            for n in range(odd * per_pair // 2, (odd + 1) * per_pair // 2)
                        ],
                        axis=0,
                    )
                    masked.append(jnp.where((spots & bit) != 0, dqs[odd], 0.0).astype(bf16))
                masked = jnp.concatenate(masked, axis=1)
                sums_p.append(mm(masked, wq))
                turned = mm(rot_ref[g].astype(bf16), masked).astype(bf16)
                turned = jnp.concatenate([turned[:, :lanes], turned[:, lanes:]], axis=0)
                turned = jnp.transpose(turned)
                for p in range(side):
                    cols = (side * g + p) * LANES
                    gq_ref[:, cols : cols + LANES] = turned[p * ROWS : (p + 1) * ROWS]

            def merged(parts):
                other = parts[1] if len(parts) > 1 else 0.0
                return jnp.where(lower, parts[0], other)

            acck[pl.ds(start, BAND), at : at + LANES] += merged(sums_k)
            accv[pl.ds(start, BAND), at : at + LANES] += merged(sums_v)
            accp[pair * head : (pair + 1) * head] += merged(sums_p)

    @pl.when(b < WINDOW // ROWS)
    def _():
        body(True)

    @pl.when(b >= WINDOW // ROWS)
    def _():
        body(False)

    @pl.when(b == last)
    def _():
        scale = head**-0.5
        lower = iota((1, LANES), 1) < head
        bytes_all = jnp.concatenate([halo_ref[:, 2 * width :], word_bytes(kw_ref[...])], axis=0)
        flags = byte_flags(bytes_all, width)
        gk = acck[...] * scale
        masked = jnp.where(flags, gk, 0.0).astype(bf16)
        for pair in range(pairs):
            at = pair * LANES
            both = mm_tn(masked[:, at : at + LANES], kn[:, at : at + LANES]) * (1.0 / scale)
            pay_ref[pair * head : (pair + 1) * head] = accp[
                pair * head : (pair + 1) * head
            ] + jnp.where(lower, both[:head], both[head:])
        seg = (iota((lanes, LANES), 0) // ROWS == iota((lanes, LANES), 1)).astype(f32)
        pay_ref[pairs * head :] = lax.dot_general(
            accs[...],
            seg,
            (((1,), (0,)), ((), ())),
            precision=lax.Precision.HIGHEST,
            preferred_element_type=f32,
        )
        ret_ref[:, :width] = gk[:WINDOW].astype(bf16)
        ret_ref[:, width:] = accv[:WINDOW].astype(bf16)
        dk_ref[...] = gk[WINDOW:]
        dv_ref[...] = accv[WINDOW:]


def keys_kernel(dk_ref, dv_ref, back_ref, kw_ref, rot_ref, kgr_ref, vg_ref):
    rows, width = dk_ref.shape
    head = LANES // 2
    edge = rows - WINDOW
    back = back_ref[...].astype(f32)
    gk = jnp.concatenate([dk_ref[:edge], dk_ref[edge:] + back[:, :width]], axis=0)
    flags = byte_flags(word_bytes(kw_ref[...]), width)
    masked = jnp.where(flags, gk, 0.0).astype(bf16)
    zero = jnp.zeros((head, head), bf16)
    for pair in range(width // LANES):
        at = pair * LANES
        turn = jnp.concatenate(
            [
                jnp.concatenate([rot_ref[2 * pair].astype(bf16), zero], axis=1),
                jnp.concatenate([zero, rot_ref[2 * pair + 1].astype(bf16)], axis=1),
            ],
            axis=0,
        )
        kgr_ref[:, at : at + LANES] = mm_nt(masked[:, at : at + LANES], turn).astype(bf16)
    vg_ref[:edge] = dv_ref[:edge].astype(bf16)
    vg_ref[edge:] = (dv_ref[edge:] + back[:, width:]).astype(bf16)


def raw_kernel(groups, pay_ref, rot_ref, raw_ref, sq_ref):
    head = LANES // 2
    total = jnp.zeros((1, head), f32)
    for g in range(groups):
        part = pay_ref[(g // 2) * head : (g // 2 + 1) * head, :]
        part = part[:, (g % 2) * head : (g % 2 + 1) * head]
        raw = lax.dot_general(
            rot_ref[g],
            part,
            (((1,), (1,)), ((), ())),
            precision=lax.Precision.HIGHEST,
            preferred_element_type=f32,
        )
        raw_ref[g] = raw
        total = total + jnp.sum(raw * raw, axis=0, keepdims=True)
    sq_ref[...] = jnp.broadcast_to(jnp.sum(total, axis=1, keepdims=True), sq_ref.shape)


def all_sum(x, axis):
    size = lax.axis_size(axis)
    if size & (size - 1):
        return lax.psum(x, axis)
    step = 1
    while step < size:
        x = x + lax.ppermute(x, axis, [(i, i ^ step) for i in range(size)])
        step *= 2
    return x


def whole(shape):
    return pl.BlockSpec(shape, lambda *_: (0,) * len(shape))


def per_device(
    query_elements,
    query_exponents,
    key_elements,
    key_exponents,
    value_elements,
    value_exponents,
    query_clip_words,
    key_clip_words,
    sinks,
    rotation,
    output_gradient,
):
    rows, query_width = query_elements.shape
    groups, head, _ = rotation.shape
    per_group = sinks.shape[0] // groups
    real_width = groups * head
    padded = groups + groups % 2
    width = padded * head
    rot = rotation
    if padded != groups:
        spare = width - real_width

        def pad(x, unit):
            return jnp.pad(x, ((0, 0), (0, spare // unit)))

        key_elements, value_elements = pad(key_elements, 1), pad(value_elements, 1)
        key_exponents = pad(key_exponents, SHARED_EXPONENT)
        value_exponents = pad(value_exponents, SHARED_EXPONENT)
        key_clip_words = pad(key_clip_words, WORD_BITS)
        rot = jnp.pad(rotation, ((0, padded - groups), (0, 0), (0, 0)))
    pairs = width // LANES
    lanes = per_group // 2 * ROWS
    blocks = width // SHARED_EXPONENT
    words = width // WORD_BITS
    all_tokens = rows * lax.axis_size("seq")
    all_heads = sinks.shape[0] * lax.axis_size("head")
    limit_value = limit_factor * math.sqrt(all_tokens * all_heads * head)
    devices = range(lax.axis_size("seq"))
    forward = [(i - 1, i) for i in devices if i]
    backward = [(i, i - 1) for i in devices if i]

    tail = rows // WINDOW - 1
    halo = pl.pallas_call(
        halo_kernel,
        grid=(1,),
        in_specs=[
            pl.BlockSpec((WINDOW, n), lambda i: (tail, 0))
            for n in (width, blocks, width, blocks, words)
        ],
        out_specs=whole((WINDOW, 2 * width + LANES)),
        out_shape=jax.ShapeDtypeStruct((WINDOW, 2 * width + LANES), bf16),
        name="halo",
    )(key_elements, key_exponents, value_elements, value_exponents, key_clip_words)
    halo = lax.ppermute(halo, "seq", forward)

    def by_block(n):
        return pl.BlockSpec((ROWS, n), lambda b: (b, 0))

    pay_rows = pairs * head + 2 * padded
    grad_q, pay, back, grad_k, grad_v = pl.pallas_call(
        functools.partial(main_kernel, groups, per_group),
        grid=(rows // ROWS,),
        in_specs=[
            pl.BlockSpec(memory_space=pltpu.SMEM),
            by_block(query_width),
            by_block(query_width // SHARED_EXPONENT),
            by_block(query_width),
            by_block(query_width // WORD_BITS),
            whole((rows, width)),
            whole((rows, blocks)),
            whole((rows, width)),
            whole((rows, blocks)),
            whole((rows, words)),
            whole((WINDOW, 2 * width + LANES)),
            whole(rot.shape),
        ],
        out_specs=[
            by_block(query_width),
            whole((pay_rows, LANES)),
            whole((WINDOW, 2 * width)),
            whole((rows, width)),
            whole((rows, width)),
        ],
        out_shape=[
            jax.ShapeDtypeStruct((rows, query_width), bf16),
            jax.ShapeDtypeStruct((pay_rows, LANES), f32),
            jax.ShapeDtypeStruct((WINDOW, 2 * width), bf16),
            jax.ShapeDtypeStruct((rows, width), f32),
            jax.ShapeDtypeStruct((rows, width), f32),
        ],
        scratch_shapes=[
            pltpu.VMEM((rows + WINDOW, width), bf16),
            pltpu.VMEM((groups, rows + WINDOW, LANES), bf16),
            pltpu.VMEM((groups, rows + WINDOW, LANES), bf16),
            pltpu.VMEM((rows + WINDOW, width), f32),
            pltpu.VMEM((rows + WINDOW, width), f32),
            pltpu.VMEM((pairs * head, LANES), f32),
            pltpu.VMEM((2 * padded, lanes), f32),
            pltpu.VMEM((2 * padded, lanes), f32),
            pltpu.VMEM((ROWS, lanes), bf16),
        ],
        compiler_params=pltpu.CompilerParams(vmem_limit_bytes=48 * 1024 * 1024),
        name="attend",
    )(
        sinks,
        query_elements,
        query_exponents,
        output_gradient,
        query_clip_words,
        key_elements,
        key_exponents,
        value_elements,
        value_exponents,
        key_clip_words,
        halo,
        rot,
    )
    pay = all_sum(pay, "seq")
    back = lax.ppermute(back, "seq", backward)
    key_gradient_raw, value_gradient = pl.pallas_call(
        keys_kernel,
        out_shape=[
            jax.ShapeDtypeStruct((rows, width), bf16),
            jax.ShapeDtypeStruct((rows, width), bf16),
        ],
        name="keys",
    )(grad_k, grad_v, back, key_clip_words, rot)
    raw, square = pl.pallas_call(
        functools.partial(raw_kernel, groups),
        out_shape=[
            jax.ShapeDtypeStruct((groups, head, head), f32),
            jax.ShapeDtypeStruct((8, LANES), f32),
        ],
        name="raw",
    )(pay, rotation)
    square = all_sum(square, "head")[0, 0]
    grad_rotation = raw * (clip_scale / jnp.maximum(jnp.sqrt(square), limit_value))
    sink_sum = pay[pairs * head : pairs * head + 2 * groups, : per_group // 2]
    sink_sum = sink_sum.reshape(groups, 2, per_group // 2).transpose(0, 2, 1).reshape(-1)
    return (
        grad_q,
        key_gradient_raw[:, :real_width],
        value_gradient[:, :real_width],
        grad_rotation,
        sink_sum,
    )


def solution(mesh):
    return jax.shard_map(
        per_device,
        mesh=mesh,
        in_specs=(
            P("seq", "head"),
            P("seq", "head"),
            P("seq", "head"),
            P("seq", "head"),
            P("seq", "head"),
            P("seq", "head"),
            P("seq", "head"),
            P("seq", "head"),
            P("head"),
            P("head", None, None),
            P("seq", "head"),
        ),
        out_specs=(
            P("seq", "head"),
            P("seq", "head"),
            P("seq", "head"),
            P("head", None, None),
            P("head"),
        ),
        check_vma=False,
    )
```

time: 387 us -> 109 us (0.28)
  matrix products: 123 us -> 0 us
  waiting for transfers between devices: 96.5 us -> 11.2 us
  Pallas kernels: 0 us -> 63.8 us
  blocking collectives: 53.7 us -> 0 us
  local copies, waits for them, and re-layouts: 51.3 us -> 11.4 us
  other arithmetic: 22.9 us -> 2.91 us
  between operations: 15.3 us -> 1.5 us
  loops' own time: 5.49 us -> 0 us
    dot_general x56 -> x0, matrix products: 123 us -> none  [the longest x8 21.3 us: attend(): jnp.einsum('igqd,jgd->gqij', dout_blk, values, preferred_element_type=jnp...]
    psum x1 -> x0, waiting for transfers between devices: 96.5 us -> none  [per_device(): summed, sink_sum = lax.psum((partial_value, sink_part), 'seq')]
    pallas_call x0 -> x4, Pallas kernels: none -> 63.8 us  [the longest x1 56.5 us: per_device(): pl.pallas_call(functools.partial(main_kernel, groups, per_group), grid=(r...]
    psum x2 -> x0, blocking collectives: 53.7 us -> none  [the longest x1 50.7 us: per_device(): summed, sink_sum = lax.psum((partial_value, sink_part), 'seq')]
    slice x11 -> x2, local copies, waits for them, and re-layouts: 19.5 us -> 1.2 us  [the longest x1 0.68 us: per_device(): sink_sum = pay[pairs * head:pairs * head + 2 * groups, :per_group // 2]]
    unnamed x63 -> x24, local copies, waits for them, and re-layouts: 23.9 us -> 9.44 us
    ppermute x7, waiting for transfers between devices: 0.02 us -> 11.2 us  [the longest x5 8.61 us: all_sum(): x = x + lax.ppermute(x, axis, [(i, i ^ step) for i in range(size)])]
    reduce_sum x18 -> x0, other arithmetic: 9.98 us -> none  [the longest x8 8.59 us: attend(): jnp.sum(numerators, axis=3) + jnp.exp(sink_logit[:, :, None] - row_max)]
  transfers between devices with their start and end apart: 8 -> 7, of which waited for: 1 -> 5; matrix products, arithmetic and copies ran while one was open for 47% -> 3% of each run, Pallas kernels for 0% -> 5%
where the time goes in v1:
time: 109 us; the launch traced here: 108 us
  Pallas kernels  63.8 us (59%)
  starting transfers between devices  17.7 us (16%)
  local copies, waits for them, and re-layouts  11.4 us (10%)
  waiting for transfers between devices  11.2 us (10%)
  other arithmetic  2.91 us (3%)
  between operations  1.5 us (1%)
    pallas_call x1, Pallas kernels, per_device(): pl.pallas_call(functools.partial(main_kernel, groups, per_group), grid=(r...  56.5 us
    ppermute x5, starting transfers between devices, all_sum(): x = x + lax.ppermute(x, axis, [(i, i ^ step) for i in range(size)])  11.5 us
    unnamed x24, local copies, waits for them, and re-layouts  9.44 us
    ppermute x5, waiting for transfers between devices, all_sum(): x = x + lax.ppermute(x, axis, [(i, i ^ step) for i in range(size)])  8.61 us
    ppermute x1, starting transfers between devices, per_device(): halo = lax.ppermute(halo, 'seq', forward)  4.86 us
    pallas_call x1, Pallas kernels, per_device(): pl.pallas_call(keys_kernel, out_shape=[jax.ShapeDtypeStruct((rows, width)...  3.47 us
    ppermute x1, waiting for transfers between devices, per_device(): halo = lax.ppermute(halo, 'seq', forward)  2.6 us
  transfers between devices with their start and end apart: 7, of which 5 were waited for; matrix products, arithmetic and copies ran while one was open for 3% of the time, Pallas kernels for 5%

profile of v1, /device:TPU:0, one launch (start us, length us, event | category | flops | bytes accessed | tf_op | source)
XLA Modules:
  0.0 108.5 jit_solution(677952927463033616)
XLA Ops:
  0.6 0.0 copy-start.4
  0.6 0.0 copy-start.3
  0.7 0.0 copy-start.5
  0.7 0.0 copy-start.8
  0.7 0.0 copy-start.7
  0.7 2.0 %copy.31.w_ref.kw_ref = s32[1024,16]{1,0:T(8,128)} copy(s32[1024,16]{0,1:T(8,128)} %param.18) | data formatting | bytes 131072 | tf_op args[7]
  2.6 0.0 copy-start
  2.7 1.8 %copy.29.ke_ref = s32[1024,8]{1,0:T(8,128)} copy(s32[1024,8]{0,1:T(8,128)} %param.14) | data formatting | bytes 65536 | tf_op args[3]
  4.5 0.0 copy-start.1
  4.5 1.8 %copy.30.ve_ref = s32[1024,8]{1,0:T(8,128)} copy(s32[1024,8]{0,1:T(8,128)} %param.16) | data formatting | bytes 65536 | tf_op args[5]
  6.3 1.8 %halo.1 = bf16[128,640]{1,0:T(8,128)(2,1)} custom-call(bf16[1024,256]{1,0:T(8,128)(2,1)} %k_ref.3, s32[1024,8]{1,0:T(8,128)} %copy.29.ke_ref, bf16[1024,256]{1,0:T(8,128)(2,1)} %v_ref.3, s32[1024,8]{1,0:T(8,128)} %copy.30.ve_ref, s32[1024,16]{1,0:T(8,128)} %copy.31.w_ref.kw_ref), custom_call_target="tpu_custom_call" | custom-call | tf_op jit(solution)/shard_map/halo/pallas_call | solution.py:379
  8.1 4.9 %collective-permute-start = (bf16[128,640]{1,0:T(8,128)(2,1)}, bf16[128,640]{1,0:T(8,128)(2,1)S(1)}, u32[]{:S(2)}, u32[]{:S(2)}) collective-permute-start(bf16[128,640]{1,0:T(8,128)(2,1)} %halo.1), channel_id=1, source_target_pairs={{0,2},{2,4},{4,6},{6,8},{8,10},{10,12},{12,14},{14,16},{16,18},{18... | collective-permute-start | bytes 491528 | tf_op jit(solution)/shard_map/ppermute | solution.py:390
  13.0 1.1 %copy.28.qe_ref = s32[1024,64]{1,0:T(8,128)S(1)} copy(s32[1024,64]{0,1:T(8,128)} %param.12) | data formatting | bytes 524288 | tf_op args[1]
  14.1 2.6 %collective-permute-done.halo_ref = bf16[128,640]{1,0:T(8,128)(2,1)S(1)} collective-permute-done((bf16[128,640]{1,0:T(8,128)(2,1)}, bf16[128,640]{1,0:T(8,128)(2,1)S(1)}, u32[]{:S(2)}, u32[]{:S(2)}) %collective-permute-start) | collective-permute-done | bytes 163872 | tf_op jit(solution)/shard_map/ppermute | solution.py:390
  16.7 0.0 copy-done.4
  16.7 0.0 copy-done.3
  16.7 0.0 copy-done.5
  16.7 0.0 copy-done.8
  16.7 0.0 copy-done.7
  16.8 0.0 copy-done
  16.8 0.0 copy-done.1
  16.8 0.0 copy-start.2
  16.8 1.0 copy-done.2
  17.8 56.5 %attend.1 = (bf16[1024,2048]{1,0:T(8,128)(2,1)}, f32[136,128]{1,0:T(8,128)S(1)}, bf16[128,512]{1,0:T(8,128)(2,1)}, f32[1024,256]{1,0:T(8,128)S(1)}, f32[1024,256]{1,0:T(8,128)}) custom-call(f32[32]{0:T(128)S(1)} %copy-done.8, bf16[1024,2048]{1,0:T(8,128)(2,1)} %q_ref.1, s32[1024,64]{1,0:T(8,128)S(1)} %copy.28.qe_ref, bf16[1024,2048]{1,0:T(8,128)(2,1)} %do_ref.1, ...), custom_call_target="tpu_custom_call" | custom-call | tf_op jit(solution)/shard_map/attend/pallas_call | solution.py:396
  74.3 0.0 copy-start.6
  74.3 1.0 copy-done.6
  75.3 2.4 %collective-permute-start.2 = (f32[136,128]{1,0:T(8,128)S(1)}, f32[136,128]{1,0:T(8,128)S(1)}, u32[]{:S(2)}, u32[]{:S(2)}) collective-permute-start(f32[136,128]{1,0:T(8,128)S(1)} %get-tuple-element.20), channel_id=1, source_target_pairs={{0,2},{2,0},{4,6},{6,4},{8,10},{10,8},{12,14},{14,12},{16,18},{18,... | collective-permute-start | bytes 208904 | tf_op jit(solution)/shard_map/ppermute | solution.py:327
  77.7 2.3 %collective-permute-done.2 = f32[136,128]{1,0:T(8,128)S(1)} collective-permute-done((f32[136,128]{1,0:T(8,128)S(1)}, f32[136,128]{1,0:T(8,128)S(1)}, u32[]{:S(2)}, u32[]{:S(2)}) %collective-permute-start.2) | collective-permute-done | bytes 69664 | tf_op jit(solution)/shard_map/ppermute | solution.py:327
  80.0 3.0 %collective-permute-start.3 = (f32[136,128]{1,0:T(8,128)S(1)}, f32[136,128]{1,0:T(8,128)S(1)}, u32[]{:S(2)}, u32[]{:S(2)}) collective-permute-start(f32[136,128]{1,0:T(8,128)S(1)} %add.15), channel_id=1, source_target_pairs={{0,4},{2,6},{4,0},{6,2},{8,12},{10,14},{12,8},{14,10},{16,20},{18,... | collective-permute-start | bytes 208904 | tf_op jit(solution)/shard_map/ppermute | solution.py:327
  83.0 2.3 %collective-permute-done.3 = f32[136,128]{1,0:T(8,128)S(1)} collective-permute-done((f32[136,128]{1,0:T(8,128)S(1)}, f32[136,128]{1,0:T(8,128)S(1)}, u32[]{:S(2)}, u32[]{:S(2)}) %collective-permute-start.3) | collective-permute-done | bytes 69664 | tf_op jit(solution)/shard_map/ppermute | solution.py:327
  85.3 3.0 %collective-permute-start.4 = (f32[136,128]{1,0:T(8,128)S(1)}, f32[136,128]{1,0:T(8,128)S(1)}, u32[]{:S(2)}, u32[]{:S(2)}) collective-permute-start(f32[136,128]{1,0:T(8,128)S(1)} %add.16), channel_id=1, source_target_pairs={{0,8},{2,10},{4,12},{6,14},{8,0},{10,2},{12,4},{14,6},{16,24},{18,... | collective-permute-start | bytes 208904 | tf_op jit(solution)/shard_map/ppermute | solution.py:327
  88.4 1.3 %collective-permute-start.1 = (bf16[128,512]{1,0:T(8,128)(2,1)}, bf16[128,512]{1,0:T(8,128)(2,1)S(1)}, u32[]{:S(2)}, u32[]{:S(2)}) collective-permute-start(bf16[128,512]{1,0:T(8,128)(2,1)} %get-tuple-element.17), channel_id=1, source_target_pairs={{2,0},{4,2},{6,4},{8,6},{10,8},{12,10},{14,12},{16,14},{18,16},{20... | collective-permute-start | bytes 393224 | tf_op jit(solution)/shard_map/ppermute | solution.py:455
  89.6 1.7 %collective-permute-done.4 = f32[136,128]{1,0:T(8,128)S(1)} collective-permute-done((f32[136,128]{1,0:T(8,128)S(1)}, f32[136,128]{1,0:T(8,128)S(1)}, u32[]{:S(2)}, u32[]{:S(2)}) %collective-permute-start.4) | collective-permute-done | bytes 69664 | tf_op jit(solution)/shard_map/ppermute | solution.py:327
  91.4 3.1 %collective-permute-start.5 = (f32[136,128]{1,0:T(8,128)S(1)}, f32[136,128]{1,0:T(8,128)S(1)}, u32[]{:S(2)}, u32[]{:S(2)}) collective-permute-start(f32[136,128]{1,0:T(8,128)S(1)} %add.17), channel_id=1, source_target_pairs={{0,16},{2,18},{4,20},{6,22},{8,24},{10,26},{12,28},{14,30},{16,0},... | collective-permute-start | bytes 208904 | tf_op jit(solution)/shard_map/ppermute | solution.py:327
  94.5 2.3 %collective-permute-done.5 = f32[136,128]{1,0:T(8,128)S(1)} collective-permute-done((f32[136,128]{1,0:T(8,128)S(1)}, f32[136,128]{1,0:T(8,128)S(1)}, u32[]{:S(2)}, u32[]{:S(2)}) %collective-permute-start.5) | collective-permute-done | bytes 69664 | tf_op jit(solution)/shard_map/ppermute | solution.py:327
  96.8 0.6 add.18.pay_ref
  97.4 2.0 %raw.1 = (f32[4,64,64]{2,1,0:T(8,128)}, f32[8,128]{1,0:T(8,128)}) custom-call(f32[136,128]{1,0:T(8,128)} %add.18.pay_ref, f32[4,64,64]{2,1,0:T(8,128)} %rot_ref.5), custom_call_target="tpu_custom_call" | custom-call | tf_op jit(solution)/shard_map/raw/pallas_call | solution.py:464
  99.4 0.0 collective-permute-start.6
  99.4 0.0 collective-permute-done.1.back_ref
  99.4 0.6 copy-done.9
  100.1 3.5 %keys.1 = (bf16[1024,256]{1,0:T(8,128)(2,1)}, bf16[1024,256]{1,0:T(8,128)(2,1)}) custom-call(f32[1024,256]{1,0:T(8,128)} %copy-done.6, f32[1024,256]{1,0:T(8,128)} %get-tuple-element.16.dv_ref, bf16[128,512]{1,0:T(8,128)(2,1)} %copy-done.9, s32[1024,16]{1,0:T(8,128)} %copy.31.w_ref.kw_ref, f32[4,64,64]{2,1,0:T(8,128)} %rot_ref.5), custom_call_target="tpu_custom_call" | custom-call | tf_op jit(solution)/shard_map/keys/pallas_call | solution.py:456
  103.6 0.7 slice.8
  104.3 0.1 copy.33
  104.4 0.6 reshape.22
  105.0 0.0 collective-permute-done.6
  105.0 0.7 add.19
  105.7 0.5 slice.6
  106.9 1.6 %broadcast_multiply_fusion = f32[4,64,64]{2,1,0:T(8,128)} fusion(f32[4,64,64]{2,1,0:T(8,128)} %get-tuple-element.21, f32[]{:T(128)} %bitcast), kind=kLoop, calls=%fused_computation | loop fusion | flops 16384 | bytes 131076 | tf_op jit(solution)/shard_map/mul | solution.py:473
  (4 shorter events, 0.0 us)
Async XLA Ops:
  0.6 16.1 %copy-start.4 = (bf16[1024,256]{1,0:T(8,128)(2,1)S(1)}, bf16[1024,256]{1,0:T(8,128)(2,1)}, u32[]{:S(2)}) copy-start(bf16[1024,256]{1,0:T(8,128)(2,1)} %v_ref.3) | copy-start | bytes 1572868
  0.6 16.1 %copy-start.3 = (bf16[1024,256]{1,0:T(8,128)(2,1)S(1)}, bf16[1024,256]{1,0:T(8,128)(2,1)}, u32[]{:S(2)}) copy-start(bf16[1024,256]{1,0:T(8,128)(2,1)} %k_ref.3) | copy-start | bytes 1572868
  0.7 16.1 %copy-start.5 = (f32[4,64,64]{2,1,0:T(8,128)S(1)}, f32[4,64,64]{2,1,0:T(8,128)}, u32[]{:S(2)}) copy-start(f32[4,64,64]{2,1,0:T(8,128)} %rot_ref.5) | copy-start | bytes 196612
  0.7 16.1 %copy-start.8 = (f32[32]{0:T(128)S(1)}, f32[32]{0:T(128)}, u32[]{:S(2)}) copy-start(f32[32]{0:T(128)} %sink_ref.1) | copy-start | bytes 388
  0.7 16.1 %copy-start.7 = (s32[1024,128]{1,0:T(8,128)S(1)}, s32[1024,128]{1,0:T(8,128)}, u32[]{:S(2)}) copy-start(s32[1024,128]{1,0:T(8,128)} %qw_ref.1) | copy-start | bytes 1572868
  2.6 14.1 %copy-start = (s32[1024,16]{1,0:T(8,128)S(1)}, s32[1024,16]{1,0:T(8,128)}, u32[]{:S(2)}) copy-start(s32[1024,16]{1,0:T(8,128)} %copy.31.w_ref.kw_ref) | copy-start | bytes 196612
  4.5 12.3 %copy-start.1 = (s32[1024,8]{1,0:T(8,128)S(1)}, s32[1024,8]{1,0:T(8,128)}, u32[]{:S(2)}) copy-start(s32[1024,8]{1,0:T(8,128)} %copy.29.ke_ref) | copy-start | bytes 98308
  8.1 8.6 %collective-permute-start = (bf16[128,640]{1,0:T(8,128)(2,1)}, bf16[128,640]{1,0:T(8,128)(2,1)S(1)}, u32[]{:S(2)}, u32[]{:S(2)}) collective-permute-start(bf16[128,640]{1,0:T(8,128)(2,1)} %halo.1), channel_id=1, source_target_pairs={{0,2},{2,4},{4,6},{6,8},{8,10},{10,12},{12,14},{14,16},{16,18},{18... | collective-permute-start | bytes 491528 | tf_op jit(solution)/shard_map/ppermute | solution.py:390
  16.8 1.0 copy-start.2
  74.3 1.0 copy-start.6
  75.3 4.7 %collective-permute-start.2 = (f32[136,128]{1,0:T(8,128)S(1)}, f32[136,128]{1,0:T(8,128)S(1)}, u32[]{:S(2)}, u32[]{:S(2)}) collective-permute-start(f32[136,128]{1,0:T(8,128)S(1)} %get-tuple-element.20), channel_id=1, source_target_pairs={{0,2},{2,0},{4,6},{6,4},{8,10},{10,8},{12,14},{14,12},{16,18},{18,... | collective-permute-start | bytes 208904 | tf_op jit(solution)/shard_map/ppermute | solution.py:327
  80.0 5.3 %collective-permute-start.3 = (f32[136,128]{1,0:T(8,128)S(1)}, f32[136,128]{1,0:T(8,128)S(1)}, u32[]{:S(2)}, u32[]{:S(2)}) collective-permute-start(f32[136,128]{1,0:T(8,128)S(1)} %add.15), channel_id=1, source_target_pairs={{0,4},{2,6},{4,0},{6,2},{8,12},{10,14},{12,8},{14,10},{16,20},{18,... | collective-permute-start | bytes 208904 | tf_op jit(solution)/shard_map/ppermute | solution.py:327
  85.3 6.1 %collective-permute-start.4 = (f32[136,128]{1,0:T(8,128)S(1)}, f32[136,128]{1,0:T(8,128)S(1)}, u32[]{:S(2)}, u32[]{:S(2)}) collective-permute-start(f32[136,128]{1,0:T(8,128)S(1)} %add.16), channel_id=1, source_target_pairs={{0,8},{2,10},{4,12},{6,14},{8,0},{10,2},{12,4},{14,6},{16,24},{18,... | collective-permute-start | bytes 208904 | tf_op jit(solution)/shard_map/ppermute | solution.py:327
  88.4 11.1 %collective-permute-start.1 = (bf16[128,512]{1,0:T(8,128)(2,1)}, bf16[128,512]{1,0:T(8,128)(2,1)S(1)}, u32[]{:S(2)}, u32[]{:S(2)}) collective-permute-start(bf16[128,512]{1,0:T(8,128)(2,1)} %get-tuple-element.17), channel_id=1, source_target_pairs={{2,0},{4,2},{6,4},{8,6},{10,8},{12,10},{14,12},{16,14},{18,16},{20... | collective-permute-start | bytes 393224 | tf_op jit(solution)/shard_map/ppermute | solution.py:455
  91.4 5.4 %collective-permute-start.5 = (f32[136,128]{1,0:T(8,128)S(1)}, f32[136,128]{1,0:T(8,128)S(1)}, u32[]{:S(2)}, u32[]{:S(2)}) collective-permute-start(f32[136,128]{1,0:T(8,128)S(1)} %add.17), channel_id=1, source_target_pairs={{0,16},{2,18},{4,20},{6,22},{8,24},{10,26},{12,28},{14,30},{16,0},... | collective-permute-start | bytes 208904 | tf_op jit(solution)/shard_map/ppermute | solution.py:327
  99.4 5.5 %collective-permute-start.6 = (f32[8,128]{1,0:T(8,128)}, f32[8,128]{1,0:T(8,128)S(1)}, u32[]{:S(2)}, u32[]{:S(2)}) collective-permute-start(f32[8,128]{1,0:T(8,128)} %get-tuple-element.22), channel_id=1, source_target_pairs={{0,1},{1,0},{2,3},{3,2},{4,5},{5,4},{6,7},{7,6},{8,9},{9,8},{10,11... | collective-permute-start | bytes 12296 | tf_op jit(solution)/shard_map/ppermute | solution.py:327
  99.4 0.7 copy-start.9

commit v2 on v1

v2 whole, which is shorter than its diff:
```python
import functools
import math

import jax
import jax.numpy as jnp
from jax import lax
from jax.experimental import pallas as pl
from jax.experimental.pallas import tpu as pltpu
from jax.sharding import PartitionSpec as P

WINDOW = 128
SHARED_EXPONENT = 32
WORD_BITS = 16
LANES = 128
UNIT = 32
STEP = 128
BAND = WINDOW + UNIT
AHEAD = 2
LAG = 3

clip_scale = 64.0
limit_factor = 0.05
negative = -1e30

f32 = jnp.float32
bf16 = jnp.bfloat16
i32 = jnp.int32


def iota(shape, dim):
    return lax.broadcasted_iota(i32, shape, dim)


def mm(a, b):
    return lax.dot_general(a, b, (((1,), (0,)), ((), ())), preferred_element_type=f32)


def mm_nt(a, b):
    return lax.dot_general(a, b, (((1,), (1,)), ((), ())), preferred_element_type=f32)


def mm_tn(a, b):
    return lax.dot_general(a, b, (((0,), (0,)), ((), ())), preferred_element_type=f32)


def zero_one(mask):
    return mask.astype(f32).astype(bf16)


def decoded(elements, powers):
    shape = (powers.shape[0], elements.shape[1])
    spread = zero_one(iota(shape, 1) // SHARED_EXPONENT == iota(shape, 0))
    scale = mm_tn(jnp.exp2(powers.astype(f32)).astype(bf16), spread)
    return elements * scale.astype(bf16)


def word_bytes(words):
    count = words.shape[0]
    shape = (count, LANES)
    low = zero_one(iota(shape, 1) == iota(shape, 0))
    high = zero_one(iota(shape, 1) == iota(shape, 0) + count)
    first = (words & 255).astype(f32).astype(bf16)
    second = ((words >> 8) & 255).astype(f32).astype(bf16)
    return (mm_tn(first, low) + mm_tn(second, high)).astype(bf16)


def byte_flags(byte_rows, width):
    count = width // WORD_BITS
    shape = (LANES, width)
    lane, row = iota(shape, 1), iota(shape, 0)
    upper = (lane % WORD_BITS) // 8
    spread = zero_one(row == lane // WORD_BITS + upper * count)
    value = mm(byte_rows, spread).astype(i32)
    bit = jnp.left_shift(jnp.ones((1, width), i32), iota((1, width), 1) % 8)
    return (value & bit) != 0


def turn_pair(rot_ref, pair):
    first = rot_ref[2 * pair].astype(bf16)
    zero = jnp.zeros_like(first)
    second = rot_ref[2 * pair + 1].astype(bf16)
    return jnp.concatenate(
        [jnp.concatenate([first, zero], axis=1), jnp.concatenate([zero, second], axis=1)], axis=0
    )


def halo_kernel(k_ref, ke_ref, v_ref, ve_ref, w_ref, out_ref):
    width = k_ref.shape[1]
    out_ref[:, :width] = decoded(k_ref[...], ke_ref[...])
    out_ref[:, width : 2 * width] = decoded(v_ref[...], ve_ref[...])
    out_ref[:, 2 * width :] = word_bytes(w_ref[...])


def attend_step(groups, per_group, edge, refs, scratch):
    sink_ref, q_ref, qe_ref, do_ref, qw_ref, rot_ref, gq_ref = refs
    kn, kg, vg, acck, accv, accp, accs, sinks = scratch
    b = pl.program_id(0)
    side = per_group // 2
    half_lanes = side * UNIT
    lanes = 2 * half_lanes
    head = LANES // 2
    start = pl.multiple_of(b * STEP, STEP)
    words = jnp.transpose(qw_ref[...])
    scales = jnp.exp2(qe_ref[...].astype(f32))
    column = iota((UNIT, lanes), 1) % UNIT
    current = iota((UNIT, lanes), 0) <= column
    low = zero_one(iota((UNIT, lanes), 0) > column)
    lower = iota((1, LANES), 1) < head
    bit = jnp.left_shift(jnp.ones((head, 1), i32), iota((head, 1), 0) % WORD_BITS)
    per_pair = 2 * head // WORD_BITS
    per_scale = 2 * head // SHARED_EXPONENT
    shared = {}

    def turned_tile(ref, g, s):
        rows = [
            ref[s * UNIT : (s + 1) * UNIT, (side * g + p) * LANES : (side * g + p + 1) * LANES]
            for p in range(side)
        ]
        both = jnp.transpose(jnp.concatenate(rows, axis=0))
        return jnp.concatenate([both[:head], both[head:]], axis=1)

    def side_by_side(x, base, count, s):
        return jnp.concatenate(
            [
                x[base + p * count : base + (p + 1) * count, s * UNIT : (s + 1) * UNIT]
                for p in range(side)
            ],
            axis=1,
        )

    def operands(g, s):
        if (g, s) not in shared:
            scale = side_by_side(scales, g * side * per_scale, per_scale, s)
            each = per_scale // 2
            scale = jnp.concatenate(
                [
                    jnp.concatenate(
                        [
                            jnp.broadcast_to(
                                scale[odd * each + n : odd * each + n + 1],
                                (SHARED_EXPONENT, half_lanes),
                            )
                            for n in range(each)
                        ],
                        axis=0,
                    )
                    for odd in range(2)
                ],
                axis=1,
            )
            qt = turned_tile(q_ref, g, s) * scale.astype(bf16)
            shared[g, s] = (qt, turned_tile(do_ref, g, s))
        return shared[g, s]

    def pair_operands(g, s):
        other = g + 1 if g % 2 == 0 else g - 1
        mine = operands(g, s)
        theirs = operands(other, s) if other < groups else mine
        first, second = (mine, theirs) if g % 2 == 0 else (theirs, mine)
        return [jnp.concatenate([x, y], axis=0) for x, y in zip(first, second)]

    def band(s):
        return pl.ds(start + s * UNIT, BAND)

    def combined(x):
        mid = x[UNIT:WINDOW]
        return jnp.concatenate([jnp.where(current, x[WINDOW:], x[:UNIT]), mid], axis=0)

    def spread(x):
        first = x[:UNIT] * low
        return jnp.concatenate([first, x[UNIT:], x[:UNIT] - first], axis=0)

    def fetch(g, s):
        operands(g, s)
        if ("k", g // 2, s) not in shared:
            at = (g // 2) * LANES
            shared["k", g // 2, s] = jnp.transpose(kn[band(s), at : at + LANES])
        spots = side_by_side(words, g * side * per_pair, per_pair, s)
        return kg[g, band(s), :], vg[g, band(s), :], sinks[pl.ds(g, 1), :], spots

    def products(g, s, loaded):
        keys, values, _, _ = loaded
        qt, dt = operands(g, s)
        scores = mm(keys, qt)
        if edge:
            limit = jnp.where(lax.axis_index("seq") == 0, WINDOW, 0) - (start + s * UNIT)
            scores = jnp.where(iota((BAND, 1), 0) >= limit, scores, negative)
        return combined(scores), combined(mm(values, dt))

    def soft(g, s, loaded, scores, gprobs):
        sink = loaded[2]
        row_max = jnp.maximum(jnp.max(scores, axis=0, keepdims=True), sink)
        numer = jnp.exp(scores - row_max)
        sink_numer = jnp.exp(sink - row_max)
        inverse = 1.0 / (jnp.sum(numer, axis=0, keepdims=True) + sink_numer)
        weights = numer * inverse
        delta = jnp.sum(weights * gprobs, axis=0, keepdims=True)
        gscores = (weights * (gprobs - delta)).astype(bf16)
        term = sink_numer * inverse * delta
        return spread(weights.astype(bf16)), spread(gscores), term

    def gradients(g, s, probs, grads):
        ktr = shared["k", g // 2, s][(g % 2) * head : (g % 2 + 1) * head]
        both_q, both_d = pair_operands(g, s)
        return mm(ktr, grads), mm_nt(grads, both_q), mm_nt(probs, both_d)

    def clipped(g, s, loaded, dq):
        spots = loaded[3]
        each = per_pair // 2
        spots = jnp.concatenate(
            [
                jnp.concatenate(
                    [
                        jnp.broadcast_to(
                            spots[odd * each + n : odd * each + n + 1], (WORD_BITS, half_lanes)
                        )
                        for n in range(each)
                    ],
                    axis=0,
                )
                for odd in range(2)
            ],
            axis=1,
        )
        masked = jnp.where((spots & bit) != 0, dq, 0.0).astype(bf16)
        turned = mm(rot_ref[g].astype(bf16), masked).astype(bf16)
        turned = jnp.concatenate([turned[:, :half_lanes], turned[:, half_lanes:]], axis=0)
        return mm_nt(masked, pair_operands(g, s)[0]), turned

    sums = {}

    def finish(g, s, term, turned, *parts):
        turned = jnp.transpose(turned)
        for p in range(side):
            cols = (side * g + p) * LANES
            gq_ref[s * UNIT : (s + 1) * UNIT, cols : cols + LANES] = turned[
                p * UNIT : (p + 1) * UNIT
            ]
        accs[pl.ds(g, 1), :] -= term
        sums[g, s] = parts
        if g % 2 == 0 and g + 1 < groups:
            return
        pair = g // 2
        at = pair * LANES
        left = sums[2 * pair, s]
        right = parts if g % 2 else (0.0, 0.0, 0.0)
        acck[band(s), at : at + LANES] += jnp.where(lower, left[0], right[0])
        accv[band(s), at : at + LANES] += jnp.where(lower, left[1], right[1])
        accp[pair * head : (pair + 1) * head] += jnp.where(lower, left[2], right[2])

    units = [
        (g, s)
        for pair in range((groups + 1) // 2)
        for s in range(STEP // UNIT)
        for g in (2 * pair, 2 * pair + 1)
        if g < groups
    ]
    loaded, ready, rounded, part, done = {}, {}, {}, {}, {}

    def stage(n, lead):
        n += lead
        return n if 0 <= n < len(units) else None

    for turn in range(-AHEAD, len(units) + LAG):
        if (n := stage(turn, AHEAD)) is not None:
            loaded[n] = fetch(*units[n])
        if (n := stage(turn, 1)) is not None:
            ready[n] = products(*units[n], loaded[n])
        if (n := stage(turn, 0)) is not None:
            rounded[n] = soft(*units[n], loaded[n], *ready.pop(n))
        if (n := stage(turn, -1)) is not None:
            part[n] = gradients(*units[n], *rounded[n][:2])
        if (n := stage(turn, -2)) is not None:
            dq, dk, dv = part.pop(n)
            dp, turned = clipped(*units[n], loaded[n], dq)
            done[n] = (rounded[n][2], turned, dk, dv, dp)
        if (n := stage(turn, -LAG)) is not None:
            finish(*units[n], *done.pop(n))


def prepare(groups, per_group, sink_ref, keys, values, scratch):
    kn, kg, vg, _, _, _, accs, sinks = scratch
    head = LANES // 2
    side = per_group // 2
    eighth = jnp.asarray(head**-0.5, bf16)
    for at, k, v in zip((0, WINDOW), keys, values):
        k = k * eighth
        kn[at : at + k.shape[0]] = k
        for g in range(groups):
            kg[g, at : at + k.shape[0]] = k[:, g * head : (g + 1) * head]
            vg[g, at : at + k.shape[0]] = v[:, g * head : (g + 1) * head]
    lanes = per_group * UNIT
    block = iota((1, lanes), 1) // UNIT
    for g in range(groups):
        row = jnp.zeros((1, lanes), f32)
        for n in range(per_group):
            h = 2 * (n % side) + n // side
            row = jnp.where(block == n, sink_ref[g * per_group + h], row)
        sinks[pl.ds(g, 1), :] = row
    accs[...] = jnp.zeros_like(accs)


def sink_sums(groups, per_group, accs):
    side = per_group // 2
    shape = (accs.shape[0], LANES)
    row, lane = iota(shape, 0), iota(shape, 1)
    total = jnp.zeros(shape, f32)
    for n in range(per_group):
        part = jnp.sum(accs[:, n * UNIT : (n + 1) * UNIT], axis=1, keepdims=True)
        h = 2 * (n % side) + n // side
        total = total + jnp.where((lane == row * per_group + h) & (row < groups), part, 0.0)
    return jnp.sum(total, axis=0, keepdims=True)


def key_terms(gk, flags, kn_rows, pair):
    at = pair * LANES
    head = LANES // 2
    masked = jnp.where(flags[:, at : at + LANES], gk[:, at : at + LANES], 0.0).astype(bf16)
    both = mm_tn(masked, kn_rows[:, at : at + LANES]) * float(head) ** 0.5
    lower = iota((1, LANES), 1) < head
    return masked, jnp.where(lower, both[:head], both[head:])


def main_kernel(
    groups,
    per_group,
    sink_ref,
    q_ref,
    qe_ref,
    do_ref,
    qw_ref,
    k_ref,
    ke_ref,
    v_ref,
    ve_ref,
    kw_ref,
    rot_ref,
    gq_ref,
    kgr_ref,
    vgr_ref,
    front_ref,
    tail_ref,
    pay_ref,
    *scratch,
):
    kn, _, _, acck, accv, accp, accs, _ = scratch
    b = pl.program_id(0)
    rows, width = k_ref.shape
    head = LANES // 2

    @pl.when(b == 0)
    def _():
        keys = decoded(k_ref[...], ke_ref[...])
        values = decoded(v_ref[...], ve_ref[...])
        prepare(groups, per_group, sink_ref, (keys,), (values,), scratch)
        acck[...] = jnp.zeros_like(acck)
        accv[...] = jnp.zeros_like(accv)
        accp[...] = jnp.zeros_like(accp)

    refs = (sink_ref, q_ref, qe_ref, do_ref, qw_ref, rot_ref, gq_ref)
    attend_step(groups, per_group, False, refs, scratch)

    @pl.when(b == pl.num_programs(0) - 1)
    def _():
        scale = head**-0.5
        front_ref[:, :width] = acck[:WINDOW]
        front_ref[:, width:] = accv[:WINDOW]
        gk = acck[WINDOW:] * scale
        gv = accv[WINDOW:]
        tail_ref[:, :width] = gk[rows - 2 * WINDOW :]
        tail_ref[:, width:] = gv[rows - 2 * WINDOW :]
        vgr_ref[WINDOW:] = gv.astype(bf16)
        flags = byte_flags(word_bytes(kw_ref[...])[WINDOW:], width)
        for pair in range(width // LANES):
            at = pair * LANES
            masked, term = key_terms(gk, flags, kn[WINDOW:], pair)
            kgr_ref[WINDOW:, at : at + LANES] = mm_nt(masked, turn_pair(rot_ref, pair)).astype(bf16)
            pay_ref[pair * head : (pair + 1) * head] = (
                accp[pair * head : (pair + 1) * head] + term
            )
        pay_ref[width // 2 :] = jnp.broadcast_to(sink_sums(groups, per_group, accs), (8, LANES))


def front_kernel(
    groups,
    per_group,
    sink_ref,
    q_ref,
    qe_ref,
    do_ref,
    qw_ref,
    k_ref,
    ke_ref,
    v_ref,
    ve_ref,
    kw_ref,
    rot_ref,
    halo_ref,
    front_ref,
    part_ref,
    gq_in,
    kgr_in,
    vgr_in,
    gq_ref,
    kgr_ref,
    vgr_ref,
    ret_ref,
    pay_ref,
    *scratch,
):
    kn, _, _, acck, accv, accp, accs, _ = scratch
    b = pl.program_id(0)
    width = k_ref.shape[1]
    head = LANES // 2

    @pl.when(b == 0)
    def _():
        keys = decoded(k_ref[...], ke_ref[...])
        values = decoded(v_ref[...], ve_ref[...])
        keys = (halo_ref[:, :width], keys)
        values = (halo_ref[:, width : 2 * width], values)
        prepare(groups, per_group, sink_ref, keys, values, scratch)
        acck[:WINDOW] = jnp.zeros((WINDOW, width), f32)
        accv[:WINDOW] = jnp.zeros((WINDOW, width), f32)
        acck[WINDOW:] = front_ref[:, :width]
        accv[WINDOW:] = front_ref[:, width:]
        accp[...] = part_ref[: width // 2]

    refs = (sink_ref, q_ref, qe_ref, do_ref, qw_ref, rot_ref, gq_ref)
    attend_step(groups, per_group, True, refs, scratch)

    @pl.when(b == pl.num_programs(0) - 1)
    def _():
        gk = acck[...] * (head**-0.5)
        ret_ref[:, :width] = gk[:WINDOW].astype(bf16)
        ret_ref[:, width:] = accv[:WINDOW].astype(bf16)
        vgr_ref[...] = accv[WINDOW:].astype(bf16)
        bytes_all = jnp.concatenate([halo_ref[:, 2 * width :], word_bytes(kw_ref[...])], axis=0)
        flags = byte_flags(bytes_all, width)
        for pair in range(width // LANES):
            at = pair * LANES
            masked, term = key_terms(gk, flags, kn[...], pair)
            kgr_ref[:, at : at + LANES] = mm_nt(
                masked[WINDOW:], turn_pair(rot_ref, pair)
            ).astype(bf16)
            pay_ref[pair * head : (pair + 1) * head] = (
                accp[pair * head : (pair + 1) * head] + term
            )
        pay_ref[width // 2 :] = part_ref[width // 2 :] + sink_sums(groups, per_group, accs)


def keys_kernel(tail_ref, back_ref, kw_ref, rot_ref, kgr_in, vgr_in, kgr_ref, vgr_ref):
    width = kgr_ref.shape[1]
    both = tail_ref[...] + back_ref[...].astype(f32)
    flags = byte_flags(word_bytes(kw_ref[...]), width)
    masked = jnp.where(flags, both[:, :width], 0.0).astype(bf16)
    for pair in range(width // LANES):
        at = pair * LANES
        kgr_ref[:, at : at + LANES] = mm_nt(
            masked[:, at : at + LANES], turn_pair(rot_ref, pair)
        ).astype(bf16)
    vgr_ref[...] = both[:, width:].astype(bf16)


def raw_kernel(groups, rot_ref, *refs):
    *pays, raw_ref, sq_ref, sink_ref = refs
    head = LANES // 2
    pay = pays[0][...]
    for x in pays[1:]:
        pay = pay + x[...]
    total = jnp.zeros((1, head), f32)
    for g in range(groups):
        part = pay[(g // 2) * head : (g // 2 + 1) * head, (g % 2) * head : (g % 2 + 1) * head]
        raw = lax.dot_general(
            rot_ref[g],
            part,
            (((1,), (1,)), ((), ())),
            precision=lax.Precision.HIGHEST,
            preferred_element_type=f32,
        )
        raw_ref[g] = raw
        total = total + jnp.sum(raw * raw, axis=0, keepdims=True)
    sq_ref[...] = jnp.broadcast_to(jnp.sum(total, axis=1, keepdims=True), sq_ref.shape)
    sink_ref[...] = pay[pay.shape[0] - 8 : pay.shape[0] - 7, : sink_ref.shape[1]]


def scale_kernel(limit_value, raw_ref, *refs):
    *squares, out_ref = refs
    square = squares[0][:1, :1]
    for x in squares[1:]:
        square = square + x[:1, :1]
    factor = clip_scale / jnp.maximum(jnp.sqrt(square), limit_value)
    for g in range(raw_ref.shape[0]):
        out_ref[g] = raw_ref[g] * factor


def addends(x, axis):
    size = lax.axis_size(axis)
    if size & (size - 1):
        return [lax.psum(x, axis)]
    step, parts = 1, [x]
    while step < size:
        x = functools.reduce(jnp.add, parts)
        masks = (step, 2 * step, 3 * step) if 2 * step < size else (step,)
        swaps = [[(i, i ^ m) for i in range(size)] for m in masks]
        parts = [x] + [lax.ppermute(x, axis, swap) for swap in swaps]
        step *= 4
    return parts


def whole(shape):
    return pl.BlockSpec(shape, lambda *_: (0,) * len(shape))


def per_device(
    query_elements,
    query_exponents,
    key_elements,
    key_exponents,
    value_elements,
    value_exponents,
    query_clip_words,
    key_clip_words,
    sinks,
    rotation,
    output_gradient,
):
    rows, query_width = query_elements.shape
    groups, head, _ = rotation.shape
    per_group = sinks.shape[0] // groups
    real_width = groups * head
    padded = groups + groups % 2
    width = padded * head
    rot = rotation
    key_powers, value_powers = key_exponents.T, value_exponents.T
    key_words = key_clip_words.T
    if padded != groups:
        spare = width - real_width
        key_elements = jnp.pad(key_elements, ((0, 0), (0, spare)))
        value_elements = jnp.pad(value_elements, ((0, 0), (0, spare)))
        key_powers = jnp.pad(key_powers, ((0, spare // SHARED_EXPONENT), (0, 0)))
        value_powers = jnp.pad(value_powers, ((0, spare // SHARED_EXPONENT), (0, 0)))
        key_words = jnp.pad(key_words, ((0, spare // WORD_BITS), (0, 0)))
        rot = jnp.pad(rotation, ((0, padded - groups), (0, 0), (0, 0)))
    lanes = per_group * UNIT
    blocks = width // SHARED_EXPONENT
    words = width // WORD_BITS
    all_tokens = rows * lax.axis_size("seq")
    all_heads = sinks.shape[0] * lax.axis_size("head")
    limit_value = limit_factor * math.sqrt(all_tokens * all_heads * head)
    devices = range(lax.axis_size("seq"))
    forward = [(i - 1, i) for i in devices if i]
    backward = [(i, i - 1) for i in devices if i]
    key_args = (key_elements, key_powers, value_elements, value_powers, key_words)

    def key_specs(count, index):
        return [
            pl.BlockSpec((count, width), lambda *_: (index, 0)),
            pl.BlockSpec((blocks, count), lambda *_: (0, index)),
            pl.BlockSpec((count, width), lambda *_: (index, 0)),
            pl.BlockSpec((blocks, count), lambda *_: (0, index)),
            pl.BlockSpec((words, count), lambda *_: (0, index)),
        ]

    last = rows // WINDOW - 1
    halo = pl.pallas_call(
        halo_kernel,
        grid=(1,),
        in_specs=key_specs(WINDOW, last),
        out_specs=whole((WINDOW, 2 * width + LANES)),
        out_shape=jax.ShapeDtypeStruct((WINDOW, 2 * width + LANES), bf16),
        name="halo",
    )(*key_args)
    halo = lax.ppermute(halo, "seq", forward)

    skip = WINDOW // STEP
    pay_rows = width // 2 + 8
    query_args = (sinks, query_elements, query_exponents.T, output_gradient, query_clip_words)

    def query_specs(offset):
        def rows_of(n):
            return pl.BlockSpec((STEP, n), lambda b: (b + offset, 0))

        powers = query_width // SHARED_EXPONENT
        return [
            pl.BlockSpec(memory_space=pltpu.SMEM),
            rows_of(query_width),
            pl.BlockSpec((powers, STEP), lambda b: (0, b + offset)),
            rows_of(query_width),
            rows_of(query_width // WORD_BITS),
        ]

    def scratch(count):
        return [
            pltpu.VMEM((count, width), bf16),
            pltpu.VMEM((groups, count, head), bf16),
            pltpu.VMEM((groups, count, head), bf16),
            pltpu.VMEM((count, width), f32),
            pltpu.VMEM((count, width), f32),
            pltpu.VMEM((width // 2, LANES), f32),
            pltpu.VMEM((8, lanes), f32),
            pltpu.VMEM((8, lanes), f32),
        ]

    params = pltpu.CompilerParams(vmem_limit_bytes=40 * 1024 * 1024)
    full_q = jax.ShapeDtypeStruct((rows, query_width), bf16)
    full_k = jax.ShapeDtypeStruct((rows, width), bf16)
    edge_f = jax.ShapeDtypeStruct((WINDOW, 2 * width), f32)
    pay_f = jax.ShapeDtypeStruct((pay_rows, LANES), f32)
    grad_q, kgr, vgr, front, tail, part = pl.pallas_call(
        functools.partial(main_kernel, groups, per_group),
        grid=(rows // STEP - skip,),
        in_specs=query_specs(skip) + key_specs(rows, 0) + [whole(rot.shape)],
        out_specs=[
            pl.BlockSpec((STEP, query_width), lambda b: (b + skip, 0)),
            whole((rows, width)),
            whole((rows, width)),
            whole((WINDOW, 2 * width)),
            whole((WINDOW, 2 * width)),
            whole((pay_rows, LANES)),
        ],
        out_shape=[full_q, full_k, full_k, edge_f, edge_f, pay_f],
        scratch_shapes=scratch(rows),
        compiler_params=params,
        cost_estimate=pl.CostEstimate(
            flops=60_000_000_000, bytes_accessed=60_000_000, transcendentals=0
        ),
        name="attend",
    )(*query_args, *key_args, rot)

    anywhere = pl.BlockSpec(memory_space=pl.ANY)
    grad_q, kgr, vgr, back, pay = pl.pallas_call(
        functools.partial(front_kernel, groups, per_group),
        grid=(skip,),
        in_specs=query_specs(0)
        + key_specs(WINDOW, 0)
        + [
            whole(rot.shape),
            whole((WINDOW, 2 * width + LANES)),
            whole((WINDOW, 2 * width)),
            whole((pay_rows, LANES)),
            anywhere,
            anywhere,
            anywhere,
        ],
        out_specs=[
            pl.BlockSpec((STEP, query_width), lambda b: (b, 0)),
            whole((WINDOW, width)),
            whole((WINDOW, width)),
            whole((WINDOW, 2 * width)),
            whole((pay_rows, LANES)),
        ],
        out_shape=[
            full_q,
            full_k,
            full_k,
            jax.ShapeDtypeStruct((WINDOW, 2 * width), bf16),
            pay_f,
        ],
        input_output_aliases={14: 0, 15: 1, 16: 2},
        scratch_shapes=scratch(2 * WINDOW),
        compiler_params=params,
        name="front",
    )(*query_args, *key_args, rot, halo, front, part, grad_q, kgr, vgr)

    pays = addends(pay, "seq")
    back = lax.ppermute(back, "seq", backward)
    kgr, vgr = pl.pallas_call(
        keys_kernel,
        grid=(1,),
        in_specs=[
            whole((WINDOW, 2 * width)),
            whole((WINDOW, 2 * width)),
            pl.BlockSpec((words, WINDOW), lambda b: (0, last)),
            whole(rot.shape),
            anywhere,
            anywhere,
        ],
        out_specs=[pl.BlockSpec((WINDOW, width), lambda b: (last, 0))] * 2,
        out_shape=[full_k, full_k],
        input_output_aliases={4: 0, 5: 1},
        cost_estimate=pl.CostEstimate(
            flops=1_000_000_000, bytes_accessed=3_000_000, transcendentals=0
        ),
        name="keys",
    )(tail, back, key_words, rot, kgr, vgr)
    raw, square, sink_sum = pl.pallas_call(
        functools.partial(raw_kernel, groups),
        out_shape=[
            jax.ShapeDtypeStruct((groups, head, head), f32),
            jax.ShapeDtypeStruct((8, LANES), f32),
            jax.ShapeDtypeStruct((1, sinks.shape[0]), f32),
        ],
        name="raw",
    )(rotation, *pays)
    grad_rotation = pl.pallas_call(
        functools.partial(scale_kernel, limit_value),
        out_shape=jax.ShapeDtypeStruct((groups, head, head), f32),
        name="scale",
    )(raw, *addends(square, "head"))
    return (
        grad_q,
        kgr[:, :real_width],
        vgr[:, :real_width],
        grad_rotation,
        sink_sum.reshape(-1),
    )


def solution(mesh):
    return jax.shard_map(
        per_device,
        mesh=mesh,
        in_specs=(
            P("seq", "head"),
            P("seq", "head"),
            P("seq", "head"),
            P("seq", "head"),
            P("seq", "head"),
            P("seq", "head"),
            P("seq", "head"),
            P("seq", "head"),
            P("head"),
            P("head", None, None),
            P("seq", "head"),
        ),
        out_specs=(
            P("seq", "head"),
            P("seq", "head"),
            P("seq", "head"),
            P("head", None, None),
            P("head"),
        ),
        check_vma=False,
    )
```

time: 109 us -> 75.2 us (0.69)
  Pallas kernels: 63.8 us -> 35.6 us
  starting transfers between devices: 17.7 us -> 14.1 us
  local copies, waits for them, and re-layouts: 11.4 us -> 14.8 us
  other arithmetic: 2.91 us -> 0.02 us
  waiting for transfers between devices: 11.2 us -> 9.2 us
    pallas_call x1, Pallas kernels: 56.5 us -> 23.3 us  [per_device(): pl.pallas_call(functools.partial(main_kernel, groups, per_group), grid=(r...]
    unnamed x24 -> x36, local copies, waits for them, and re-layouts: 9.44 us -> 14.8 us
    pallas_call x2 -> x4, Pallas kernels: 5.3 us -> 10.2 us  [the longest x1 4.59 us: per_device(): pl.pallas_call(functools.partial(front_kernel, groups, per_group), grid=(...]
    ppermute x5 -> x7, starting transfers between devices: 11.5 us -> 7.94 us  [addends(): parts = [x] + [lax.ppermute(x, axis, swap) for swap in swaps]]
    ppermute x1, waiting for transfers between devices: 2.6 us -> 0.01 us  [per_device(): halo = lax.ppermute(halo, 'seq', forward)]
    mul x1 -> x0, other arithmetic: 1.57 us -> none  [per_device(): raw * (clip_scale / jnp.maximum(jnp.sqrt(square), limit_value))]
    add x5 -> x1, other arithmetic: 1.34 us -> 0.02 us  [addends(): x = functools.reduce(jnp.add, parts)]
    slice x2 -> x0, local copies, waits for them, and re-layouts: 1.2 us -> none  [the longest x1 0.68 us: per_device(): sink_sum = pay[pairs * head:pairs * head + 2 * groups, :per_group // 2]]
  transfers between devices with their start and end apart: 7 -> 9, of which waited for: 5 -> 5; matrix products, arithmetic and copies ran while one was open for 3% -> 0% of each run, Pallas kernels for 5% -> 37%
where the time goes in v2:
time: 75.2 us; the launch traced here: 74.5 us
  Pallas kernels  35.6 us (47%)
  local copies, waits for them, and re-layouts  14.8 us (20%)
  starting transfers between devices  14.1 us (19%)
  waiting for transfers between devices  9.2 us (12%)
    pallas_call x1, Pallas kernels, per_device(): pl.pallas_call(functools.partial(main_kernel, groups, per_group), grid=(r...  23.3 us
    unnamed x36, local copies, waits for them, and re-layouts  14.8 us
    ppermute x7, waiting for transfers between devices, addends(): parts = [x] + [lax.ppermute(x, axis, swap) for swap in swaps]  9.2 us
    ppermute x7, starting transfers between devices, addends(): parts = [x] + [lax.ppermute(x, axis, swap) for swap in swaps]  7.94 us
    ppermute x1, starting transfers between devices, per_device(): halo = lax.ppermute(halo, 'seq', forward)  4.86 us
    pallas_call x1, Pallas kernels, per_device(): pl.pallas_call(functools.partial(front_kernel, groups, per_group), grid=(...  4.59 us
    pallas_call x1, Pallas kernels, per_device(): pl.pallas_call(keys_kernel, grid=(1,), in_specs=[whole((WINDOW, 2 * width...  2.16 us
    pallas_call x1, Pallas kernels, per_device(): pl.pallas_call(functools.partial(raw_kernel, groups), out_shape=[jax.Shap...  2.12 us
  transfers between devices with their start and end apart: 9, of which 5 were waited for; matrix products, arithmetic and copies ran while one was open for 0% of the time, Pallas kernels for 37%

profile of v2, /device:TPU:0, one launch (start us, length us, event | category | flops | bytes accessed | tf_op | source)
XLA Modules:
  0.0 74.5 jit_solution(9601477956675527278)
XLA Ops:
  0.6 1.8 %halo.1 = bf16[128,640]{1,0:T(8,128)(2,1)} custom-call(bf16[1024,256]{1,0:T(8,128)(2,1)} %k_ref.5, s32[8,1024]{1,0:T(8,128)} %bitcast.11, bf16[1024,256]{1,0:T(8,128)(2,1)} %v_ref.5, s32[8,1024]{1,0:T(8,128)} %bitcast.14, s32[16,1024]{1,0:T(8,128)} %bitcast.7), custom_call_target="tpu_custom_call" | custom-call | tf_op jit(solution)/shard_map/halo/pallas_call | solution.py:566
  2.5 4.9 %collective-permute-start = (bf16[128,640]{1,0:T(8,128)(2,1)}, bf16[128,640]{1,0:T(8,128)(2,1)S(1)}, u32[]{:S(2)}, u32[]{:S(2)}) collective-permute-start(bf16[128,640]{1,0:T(8,128)(2,1)} %halo.1), channel_id=1, source_target_pairs={{0,2},{2,4},{4,6},{6,8},{8,10},{10,12},{12,14},{14,16},{16,18},{18... | collective-permute-start | bytes 491528 | tf_op jit(solution)/shard_map/ppermute | solution.py:574
  7.3 0.0 copy-start
  7.3 2.2 %copy-done = bf16[1024,2048]{1,0:T(8,128)(2,1)S(1)} copy-done((bf16[1024,2048]{1,0:T(8,128)(2,1)S(1)}, bf16[1024,2048]{1,0:T(8,128)(2,1)}, u32[]{:S(2)}) %copy-start) | copy-done | bytes 4194328
  9.5 0.0 copy-start.1
  9.5 2.2 %copy-done.1 = bf16[1024,2048]{1,0:T(8,128)(2,1)S(1)} copy-done((bf16[1024,2048]{1,0:T(8,128)(2,1)S(1)}, bf16[1024,2048]{1,0:T(8,128)(2,1)}, u32[]{:S(2)}) %copy-start.1) | copy-done | bytes 4194328
  11.7 0.0 copy-start.2
  11.7 1.0 %copy-done.2 = bf16[1024,256]{1,0:T(8,128)(2,1)S(1)} copy-done((bf16[1024,256]{1,0:T(8,128)(2,1)S(1)}, bf16[1024,256]{1,0:T(8,128)(2,1)}, u32[]{:S(2)}) %copy-start.2) | copy-done | bytes 524312
  12.8 0.0 copy-start.3
  12.8 1.0 %copy-done.3 = bf16[1024,256]{1,0:T(8,128)(2,1)S(1)} copy-done((bf16[1024,256]{1,0:T(8,128)(2,1)S(1)}, bf16[1024,256]{1,0:T(8,128)(2,1)}, u32[]{:S(2)}) %copy-start.3) | copy-done | bytes 524312
  13.8 0.9 %copy-done.4 = f32[4,64,64]{2,1,0:T(8,128)S(1)} copy-done((f32[4,64,64]{2,1,0:T(8,128)S(1)}, f32[4,64,64]{2,1,0:T(8,128)}, u32[]{:S(2)}) %copy-start.4) | copy-done | bytes 65560
  14.7 1.0 %copy-done.5 = s32[1024,128]{1,0:T(8,128)S(1)} copy-done((s32[1024,128]{1,0:T(8,128)S(1)}, s32[1024,128]{1,0:T(8,128)}, u32[]{:S(2)}) %copy-start.5) | copy-done | bytes 524312
  15.8 0.9 %copy-done.6 = s32[1024,64]{0,1:T(8,128)S(1)} copy-done((s32[1024,64]{0,1:T(8,128)S(1)}, s32[1024,64]{0,1:T(8,128)}, u32[]{:S(2)}) %copy-start.6) | copy-done | bytes 262168
  16.7 0.8 %copy-done.7 = s32[1024,16]{0,1:T(8,128)S(1)} copy-done((s32[1024,16]{0,1:T(8,128)S(1)}, s32[1024,16]{0,1:T(8,128)}, u32[]{:S(2)}) %copy-start.7) | copy-done | bytes 65560
  17.5 0.8 %copy-done.8 = s32[1024,8]{0,1:T(8,128)S(1)} copy-done((s32[1024,8]{0,1:T(8,128)S(1)}, s32[1024,8]{0,1:T(8,128)}, u32[]{:S(2)}) %copy-start.8) | copy-done | bytes 32792
  18.3 0.8 %copy-done.9 = s32[1024,8]{0,1:T(8,128)S(1)} copy-done((s32[1024,8]{0,1:T(8,128)S(1)}, s32[1024,8]{0,1:T(8,128)}, u32[]{:S(2)}) %copy-start.9) | copy-done | bytes 32792
  19.1 0.7 copy-done.10
  19.7 23.3 %attend.1 = (bf16[1024,2048]{1,0:T(8,128)(2,1)}, bf16[1024,256]{1,0:T(8,128)(2,1)}, bf16[1024,256]{1,0:T(8,128)(2,1)}, f32[128,512]{1,0:T(8,128)S(1)}, f32[128,512]{1,0:T(8,128)S(1)}, /*index=5*/f32[136,128]{1,0:T(8,128)S(1)}) custom-call(f32[32]{0:T(128)S(1)} %copy-done.10, bf16[1024,2048]{1,0:T(8,128)(2,1)S(1)} %copy-done, s32[64,1024]{1,0:T(8,128)S(1)} %bitcast.5, ...), custom_call_target="tpu_custom_call" | custom-call | flops 60000002048 | bytes 60000000 | tf_op jit(solution)/shard_map/attend/pallas_call | solution.py:610
  43.0 0.0 collective-permute-done.halo_ref
  43.0 4.6 %front.1 = (bf16[1024,2048]{1,0:T(8,128)(2,1)}, bf16[1024,256]{1,0:T(8,128)(2,1)}, bf16[1024,256]{1,0:T(8,128)(2,1)}, bf16[128,512]{1,0:T(8,128)(2,1)S(1)}, f32[136,128]{1,0:T(8,128)S(1)}) custom-call(f32[32]{0:T(128)S(1)} %copy-done.10, bf16[1024,2048]{1,0:T(8,128)(2,1)S(1)} %copy-done, ...), custom_call_target="tpu_custom_call", output_to_operand_aliasing={{0}: (14, {}), {1}: (15, {}), {2}: (16, {})} | custom-call | tf_op jit(solution)/shard_map/front/pallas_call | solution.py:632
  47.6 0.0 copy-done.11
  47.6 2.5 %collective-permute-start.4 = (f32[136,128]{1,0:T(8,128)S(1)}, f32[136,128]{1,0:T(8,128)S(1)}, u32[]{:S(2)}, u32[]{:S(2)}) collective-permute-start(f32[136,128]{1,0:T(8,128)S(1)} %get-tuple-element.33), channel_id=1, source_target_pairs={{0,6},{2,4},{4,2},{6,0},{8,14},{10,12},{12,10},{14,8},{16,22},{18,... | collective-permute-start | bytes 208904 | tf_op jit(solution)/shard_map/ppermute | solution.py:506
  50.1 0.5 collective-permute-start.3
  50.6 0.5 collective-permute-start.2
  51.1 1.3 %collective-permute-start.1 = (bf16[128,512]{1,0:T(8,128)(2,1)S(1)}, bf16[128,512]{1,0:T(8,128)(2,1)S(1)}, u32[]{:S(2)}, u32[]{:S(2)}) collective-permute-start(bf16[128,512]{1,0:T(8,128)(2,1)S(1)} %get-tuple-element.28), channel_id=1, source_target_pairs={{2,0},{4,2},{6,4},{8,6},{10,8},{12,10},{14,12},{16,14},{18,16},{20... | collective-permute-start | bytes 393224 | tf_op jit(solution)/shard_map/ppermute | solution.py:667
  52.4 0.5 collective-permute-done.4
  52.9 1.4 %collective-permute-done.3 = f32[136,128]{1,0:T(8,128)S(1)} collective-permute-done((f32[136,128]{1,0:T(8,128)S(1)}, f32[136,128]{1,0:T(8,128)S(1)}, u32[]{:S(2)}, u32[]{:S(2)}) %collective-permute-start.3) | collective-permute-done | bytes 69664 | tf_op jit(solution)/shard_map/ppermute | solution.py:506
  54.4 1.1 %collective-permute-done.2 = f32[136,128]{1,0:T(8,128)S(1)} collective-permute-done((f32[136,128]{1,0:T(8,128)S(1)}, f32[136,128]{1,0:T(8,128)S(1)}, u32[]{:S(2)}, u32[]{:S(2)}) %collective-permute-start.2) | collective-permute-done | bytes 69664 | tf_op jit(solution)/shard_map/ppermute | solution.py:506
  55.5 0.0 copy-start.12
  55.5 3.7 %collective-permute-start.7 = (f32[136,128]{1,0:T(8,128)S(1)}, f32[136,128]{1,0:T(8,128)S(1)}, u32[]{:S(2)}, u32[]{:S(2)}) collective-permute-start(f32[136,128]{1,0:T(8,128)S(1)} %add_add_fusion.refs_0_), channel_id=1, source_target_pairs={{0,24},{2,26},{4,28},{6,30},{8,16},{10,18},{12,20},{14,22},{16,8},... | collective-permute-start | bytes 208904 | tf_op jit(solution)/shard_map/ppermute | solution.py:506
  59.2 0.0 collective-permute-start.6
  59.2 0.8 %collective-permute-start.5 = (f32[136,128]{1,0:T(8,128)S(1)}, f32[136,128]{1,0:T(8,128)S(1)}, u32[]{:S(2)}, u32[]{:S(2)}) collective-permute-start(f32[136,128]{1,0:T(8,128)S(1)} %add_add_fusion.refs_0_), channel_id=1, source_target_pairs={{0,8},{2,10},{4,12},{6,14},{8,0},{10,2},{12,4},{14,6},{16,24},{18,... | collective-permute-start | bytes 208904 | tf_op jit(solution)/shard_map/ppermute | solution.py:506
  60.0 4.2 %collective-permute-done.7.refs_3_ = f32[136,128]{1,0:T(8,128)S(1)} collective-permute-done((f32[136,128]{1,0:T(8,128)S(1)}, f32[136,128]{1,0:T(8,128)S(1)}, u32[]{:S(2)}, u32[]{:S(2)}) %collective-permute-start.7) | collective-permute-done | bytes 69664 | tf_op jit(solution)/shard_map/ppermute | solution.py:506
  64.1 2.0 %collective-permute-done.6.refs_2_ = f32[136,128]{1,0:T(8,128)S(1)} collective-permute-done((f32[136,128]{1,0:T(8,128)S(1)}, f32[136,128]{1,0:T(8,128)S(1)}, u32[]{:S(2)}, u32[]{:S(2)}) %collective-permute-start.6) | collective-permute-done | bytes 69664 | tf_op jit(solution)/shard_map/ppermute | solution.py:506
  66.1 0.0 collective-permute-done.5.refs_1_
  66.1 0.0 copy-done.12
  66.1 0.0 copy-done.13
  66.1 0.6 copy-done.14
  66.7 0.6 copy-done.15
  67.3 2.1 %raw.1 = (f32[4,64,64]{2,1,0:T(8,128)}, f32[8,128]{1,0:T(8,128)}, f32[1,32]{1,0:T(1,128)}) custom-call(f32[4,64,64]{2,1,0:T(8,128)} %rot_ref.7, f32[136,128]{1,0:T(8,128)} %copy-done.12, f32[136,128]{1,0:T(8,128)} %copy-done.15, f32[136,128]{1,0:T(8,128)} %copy-done.14, f32[136,128]{1,0:T(8,128)} %copy-done.13), custom_call_target="tpu_custom_call" | custom-call | tf_op jit(solution)/shard_map/raw/pallas_call | solution.py:687
  69.5 0.0 collective-permute-start.8
  69.5 0.0 collective-permute-done.1.back_ref
  69.5 0.0 copy-start.17
  69.5 0.6 copy-done.17
  70.1 2.2 %keys.1 = (bf16[1024,256]{1,0:T(8,128)(2,1)}, bf16[1024,256]{1,0:T(8,128)(2,1)}) custom-call(f32[128,512]{1,0:T(8,128)} %copy-done.11, bf16[128,512]{1,0:T(8,128)(2,1)} %copy-done.17, s32[16,1024]{1,0:T(8,128)} %bitcast.8, f32[4,64,64]{2,1,0:T(8,128)} %rot_ref.7, ...), custom_call_target="tpu_custom_call", output_to_operand_aliasing={{0}: (4, {}), {1}: (5, {})} | custom-call | flops 1000000000 | bytes 3000000 | tf_op jit(solution)/shard_map/keys/pallas_call | solution.py:668
  72.3 0.0 collective-permute-done.8.refs_1_
  72.3 0.6 copy-done.16
  72.9 1.6 %scale.1 = f32[4,64,64]{2,1,0:T(8,128)} custom-call(f32[4,64,64]{2,1,0:T(8,128)} %get-tuple-element.34.raw_ref, f32[8,128]{1,0:T(8,128)} %get-tuple-element.35.refs_0_, f32[8,128]{1,0:T(8,128)} %copy-done.16), custom_call_target="tpu_custom_call" | custom-call | tf_op jit(solution)/shard_map/scale/pallas_call | solution.py:696
  (13 shorter events, 0.0 us)
Async XLA Ops:
  2.5 40.6 %collective-permute-start = (bf16[128,640]{1,0:T(8,128)(2,1)}, bf16[128,640]{1,0:T(8,128)(2,1)S(1)}, u32[]{:S(2)}, u32[]{:S(2)}) collective-permute-start(bf16[128,640]{1,0:T(8,128)(2,1)} %halo.1), channel_id=1, source_target_pairs={{0,2},{2,4},{4,6},{6,8},{8,10},{10,12},{12,14},{14,16},{16,18},{18... | collective-permute-start | bytes 491528 | tf_op jit(solution)/shard_map/ppermute | solution.py:574
  7.3 2.2 %copy-start = (bf16[1024,2048]{1,0:T(8,128)(2,1)S(1)}, bf16[1024,2048]{1,0:T(8,128)(2,1)}, u32[]{:S(2)}) copy-start(bf16[1024,2048]{1,0:T(8,128)(2,1)} %q_ref.3) | copy-start | bytes 12582916
  9.5 2.2 %copy-start.1 = (bf16[1024,2048]{1,0:T(8,128)(2,1)S(1)}, bf16[1024,2048]{1,0:T(8,128)(2,1)}, u32[]{:S(2)}) copy-start(bf16[1024,2048]{1,0:T(8,128)(2,1)} %do_ref.3) | copy-start | bytes 12582916
  11.7 1.0 %copy-start.2 = (bf16[1024,256]{1,0:T(8,128)(2,1)S(1)}, bf16[1024,256]{1,0:T(8,128)(2,1)}, u32[]{:S(2)}) copy-start(bf16[1024,256]{1,0:T(8,128)(2,1)} %k_ref.5) | copy-start | bytes 1572868
  12.8 1.0 %copy-start.3 = (bf16[1024,256]{1,0:T(8,128)(2,1)S(1)}, bf16[1024,256]{1,0:T(8,128)(2,1)}, u32[]{:S(2)}) copy-start(bf16[1024,256]{1,0:T(8,128)(2,1)} %v_ref.5) | copy-start | bytes 1572868
  13.8 0.9 %copy-start.4 = (f32[4,64,64]{2,1,0:T(8,128)S(1)}, f32[4,64,64]{2,1,0:T(8,128)}, u32[]{:S(2)}) copy-start(f32[4,64,64]{2,1,0:T(8,128)} %rot_ref.7) | copy-start | bytes 196612
  14.7 1.0 %copy-start.5 = (s32[1024,128]{1,0:T(8,128)S(1)}, s32[1024,128]{1,0:T(8,128)}, u32[]{:S(2)}) copy-start(s32[1024,128]{1,0:T(8,128)} %qw_ref.3) | copy-start | bytes 1572868
  15.7 0.9 %copy-start.6 = (s32[1024,64]{0,1:T(8,128)S(1)}, s32[1024,64]{0,1:T(8,128)}, u32[]{:S(2)}) copy-start(s32[1024,64]{0,1:T(8,128)} %param.12) | copy-start | bytes 786436
  16.7 0.8 %copy-start.7 = (s32[1024,16]{0,1:T(8,128)S(1)}, s32[1024,16]{0,1:T(8,128)}, u32[]{:S(2)}) copy-start(s32[1024,16]{0,1:T(8,128)} %param.18) | copy-start | bytes 196612
  17.5 0.8 %copy-start.8 = (s32[1024,8]{0,1:T(8,128)S(1)}, s32[1024,8]{0,1:T(8,128)}, u32[]{:S(2)}) copy-start(s32[1024,8]{0,1:T(8,128)} %param.14) | copy-start | bytes 98308
  18.3 0.8 %copy-start.9 = (s32[1024,8]{0,1:T(8,128)S(1)}, s32[1024,8]{0,1:T(8,128)}, u32[]{:S(2)}) copy-start(s32[1024,8]{0,1:T(8,128)} %param.16) | copy-start | bytes 98308
  19.1 0.7 copy-start.10
  43.0 4.6 %copy-start.11 = (f32[128,512]{1,0:T(8,128)}, f32[128,512]{1,0:T(8,128)S(1)}, u32[]{:S(2)}) copy-start(f32[128,512]{1,0:T(8,128)S(1)} %get-tuple-element.27.tail_ref) | copy-start | bytes 786436
  47.6 5.3 %collective-permute-start.4 = (f32[136,128]{1,0:T(8,128)S(1)}, f32[136,128]{1,0:T(8,128)S(1)}, u32[]{:S(2)}, u32[]{:S(2)}) collective-permute-start(f32[136,128]{1,0:T(8,128)S(1)} %get-tuple-element.33), channel_id=1, source_target_pairs={{0,6},{2,4},{4,2},{6,0},{8,14},{10,12},{12,10},{14,8},{16,22},{18,... | collective-permute-start | bytes 208904 | tf_op jit(solution)/shard_map/ppermute | solution.py:506
  50.1 4.3 %collective-permute-start.3 = (f32[136,128]{1,0:T(8,128)S(1)}, f32[136,128]{1,0:T(8,128)S(1)}, u32[]{:S(2)}, u32[]{:S(2)}) collective-permute-start(f32[136,128]{1,0:T(8,128)S(1)} %get-tuple-element.33), channel_id=1, source_target_pairs={{0,4},{2,6},{4,0},{6,2},{8,12},{10,14},{12,8},{14,10},{16,20},{18,... | collective-permute-start | bytes 208904 | tf_op jit(solution)/shard_map/ppermute | solution.py:506
  50.6 4.9 %collective-permute-start.2 = (f32[136,128]{1,0:T(8,128)S(1)}, f32[136,128]{1,0:T(8,128)S(1)}, u32[]{:S(2)}, u32[]{:S(2)}) collective-permute-start(f32[136,128]{1,0:T(8,128)S(1)} %get-tuple-element.33), channel_id=1, source_target_pairs={{0,2},{2,0},{4,6},{6,4},{8,10},{10,8},{12,14},{14,12},{16,18},{18,... | collective-permute-start | bytes 208904 | tf_op jit(solution)/shard_map/ppermute | solution.py:506
  51.1 18.4 %collective-permute-start.1 = (bf16[128,512]{1,0:T(8,128)(2,1)S(1)}, bf16[128,512]{1,0:T(8,128)(2,1)S(1)}, u32[]{:S(2)}, u32[]{:S(2)}) collective-permute-start(bf16[128,512]{1,0:T(8,128)(2,1)S(1)} %get-tuple-element.28), channel_id=1, source_target_pairs={{2,0},{4,2},{6,4},{8,6},{10,8},{12,10},{14,12},{16,14},{18,16},{20... | collective-permute-start | bytes 393224 | tf_op jit(solution)/shard_map/ppermute | solution.py:667
  55.5 10.6 %copy-start.12 = (f32[136,128]{1,0:T(8,128)}, f32[136,128]{1,0:T(8,128)S(1)}, u32[]{:S(2)}) copy-start(f32[136,128]{1,0:T(8,128)S(1)} %add_add_fusion.refs_0_) | copy-start | bytes 208900
  55.5 8.6 %collective-permute-start.7 = (f32[136,128]{1,0:T(8,128)S(1)}, f32[136,128]{1,0:T(8,128)S(1)}, u32[]{:S(2)}, u32[]{:S(2)}) collective-permute-start(f32[136,128]{1,0:T(8,128)S(1)} %add_add_fusion.refs_0_), channel_id=1, source_target_pairs={{0,24},{2,26},{4,28},{6,30},{8,16},{10,18},{12,20},{14,22},{16,8},... | collective-permute-start | bytes 208904 | tf_op jit(solution)/shard_map/ppermute | solution.py:506
  59.2 6.9 %collective-permute-start.6 = (f32[136,128]{1,0:T(8,128)S(1)}, f32[136,128]{1,0:T(8,128)S(1)}, u32[]{:S(2)}, u32[]{:S(2)}) collective-permute-start(f32[136,128]{1,0:T(8,128)S(1)} %add_add_fusion.refs_0_), channel_id=1, source_target_pairs={{0,16},{2,18},{4,20},{6,22},{8,24},{10,26},{12,28},{14,30},{16,0},... | collective-permute-start | bytes 208904 | tf_op jit(solution)/shard_map/ppermute | solution.py:506
  59.2 6.9 %collective-permute-start.5 = (f32[136,128]{1,0:T(8,128)S(1)}, f32[136,128]{1,0:T(8,128)S(1)}, u32[]{:S(2)}, u32[]{:S(2)}) collective-permute-start(f32[136,128]{1,0:T(8,128)S(1)} %add_add_fusion.refs_0_), channel_id=1, source_target_pairs={{0,8},{2,10},{4,12},{6,14},{8,0},{10,2},{12,4},{14,6},{16,24},{18,... | collective-permute-start | bytes 208904 | tf_op jit(solution)/shard_map/ppermute | solution.py:506
  64.1 2.0 %copy-start.13 = (f32[136,128]{1,0:T(8,128)}, f32[136,128]{1,0:T(8,128)S(1)}, u32[]{:S(2)}) copy-start(f32[136,128]{1,0:T(8,128)S(1)} %collective-permute-done.7.refs_3_) | copy-start | bytes 208900
  66.1 0.6 copy-start.14
  66.7 0.6 copy-start.15
  69.5 2.8 %collective-permute-start.8 = (f32[8,128]{1,0:T(8,128)}, f32[8,128]{1,0:T(8,128)S(1)}, u32[]{:S(2)}, u32[]{:S(2)}) collective-permute-start(f32[8,128]{1,0:T(8,128)} %get-tuple-element.35.refs_0_), channel_id=1, source_target_pairs={{0,1},{1,0},{2,3},{3,2},{4,5},{5,4},{6,7},{7,6},{8,9},{9,8},{10,11... | collective-permute-start | bytes 12296 | tf_op jit(solution)/shard_map/ppermute | solution.py:506
  69.5 0.7 copy-start.17
  72.3 0.6 copy-start.16

commit v3 on v2

--- a/solution.py
+++ b/solution.py
@@ -7,6 +7,7 @@
 from jax.experimental import pallas as pl
 from jax.experimental.pallas import tpu as pltpu
 from jax.sharding import PartitionSpec as P
+
 
 WINDOW = 128
 SHARED_EXPONENT = 32
@@ -92,7 +93,7 @@
 
 
 def attend_step(groups, per_group, edge, refs, scratch):
-    sink_ref, q_ref, qe_ref, do_ref, qw_ref, rot_ref, gq_ref = refs
+    _, q_ref, qe_ref, do_ref, qw_ref, rot_ref, gq_ref = refs
     kn, kg, vg, acck, accv, accp, accs, sinks = scratch
     b = pl.program_id(0)
     side = per_group // 2
@@ -378,7 +379,7 @@
             pay_ref[pair * head : (pair + 1) * head] = (
                 accp[pair * head : (pair + 1) * head] + term
             )
-        pay_ref[width // 2 :] = jnp.broadcast_to(sink_sums(groups, per_group, accs), (8, LANES))
+        pay_ref[width // 2 :] = jnp.broadcast_to(sink_sums(groups, per_group, accs), (16, LANES))
 
 
 def front_kernel(
@@ -406,6 +407,7 @@
     vgr_ref,
     ret_ref,
     pay_ref,
+    send_ref,
     *scratch,
 ):
     kn, _, _, acck, accv, accp, accs, _ = scratch
@@ -446,7 +448,14 @@
             pay_ref[pair * head : (pair + 1) * head] = (
                 accp[pair * head : (pair + 1) * head] + term
             )
-        pay_ref[width // 2 :] = part_ref[width // 2 :] + sink_sums(groups, per_group, accs)
+        sink = part_ref[width // 2 : width // 2 + 1] + sink_sums(groups, per_group, accs)
+        tail_row = iota((16, LANES), 0)
+        pay_ref[width // 2 :] = jnp.where(tail_row == 0, sink, 0.0)
+        send_ref[: width // 2] = pay_ref[: width // 2].astype(bf16)
+        rest = sink - sink.astype(bf16).astype(f32)
+        send_ref[width // 2 :] = jnp.where(
+            tail_row == 0, sink, jnp.where(tail_row == 1, rest, 0.0)
+        ).astype(bf16)
 
 
 def keys_kernel(tail_ref, back_ref, kw_ref, rot_ref, kgr_in, vgr_in, kgr_ref, vgr_ref):
@@ -467,7 +476,7 @@
     head = LANES // 2
     pay = pays[0][...]
     for x in pays[1:]:
-        pay = pay + x[...]
+        pay = pay + x[...].astype(f32)
     total = jnp.zeros((1, head), f32)
     for g in range(groups):
         part = pay[(g // 2) * head : (g // 2 + 1) * head, (g % 2) * head : (g % 2 + 1) * head]
@@ -481,7 +490,8 @@
         raw_ref[g] = raw
         total = total + jnp.sum(raw * raw, axis=0, keepdims=True)
     sq_ref[...] = jnp.broadcast_to(jnp.sum(total, axis=1, keepdims=True), sq_ref.shape)
-    sink_ref[...] = pay[pay.shape[0] - 8 : pay.shape[0] - 7, : sink_ref.shape[1]]
+    at = pay.shape[0] - 16
+    sink_ref[...] = (pay[at : at + 1] + pay[at + 1 : at + 2])[:, : sink_ref.shape[1]]
 
 
 def scale_kernel(limit_value, raw_ref, *refs):
@@ -494,25 +504,37 @@
         out_ref[g] = raw_ref[g] * factor
 
 
-def addends(x, axis):
+def addends(x, axis, send=None, pack=None):
     size = lax.axis_size(axis)
     if size & (size - 1):
         return [lax.psum(x, axis)]
     step, parts = 1, [x]
     while step < size:
-        x = functools.reduce(jnp.add, parts)
+        if step > 1:
+            x = functools.reduce(jnp.add, [part.astype(f32) for part in parts])
+            send = None if pack is None else pack(x)
         masks = (step, 2 * step, 3 * step) if 2 * step < size else (step,)
         swaps = [[(i, i ^ m) for i in range(size)] for m in masks]
-        parts = [x] + [lax.ppermute(x, axis, swap) for swap in swaps]
+        out = x if send is None else send
+        parts = [x]
+        for swap in swaps:
+            parts.append(lax.ppermute(out, axis, swap))
         step *= 4
     return parts
 
 
+def packed(rows, x):
+    rest = x - lax.reduce_precision(x, 8, 7)
+    moved = jnp.concatenate([rest[-1:], rest[:-1]], axis=0)
+    row = iota(x.shape, 0)
+    return jnp.where(row == rows + 1, x + moved, x).astype(bf16)
+
+
 def whole(shape):
     return pl.BlockSpec(shape, lambda *_: (0,) * len(shape))
 
 
-def per_device(
+def device_work(
     query_elements,
     query_exponents,
     key_elements,
@@ -574,7 +596,7 @@
     halo = lax.ppermute(halo, "seq", forward)
 
     skip = WINDOW // STEP
-    pay_rows = width // 2 + 8
+    pay_rows = width // 2 + 16
     query_args = (sinks, query_elements, query_exponents.T, output_gradient, query_clip_words)
 
     def query_specs(offset):
@@ -602,7 +624,7 @@
             pltpu.VMEM((8, lanes), f32),
         ]
 
-    params = pltpu.CompilerParams(vmem_limit_bytes=40 * 1024 * 1024)
+    params = pltpu.CompilerParams(vmem_limit_bytes=67043328)
     full_q = jax.ShapeDtypeStruct((rows, query_width), bf16)
     full_k = jax.ShapeDtypeStruct((rows, width), bf16)
     edge_f = jax.ShapeDtypeStruct((WINDOW, 2 * width), f32)
@@ -629,7 +651,7 @@
     )(*query_args, *key_args, rot)
 
     anywhere = pl.BlockSpec(memory_space=pl.ANY)
-    grad_q, kgr, vgr, back, pay = pl.pallas_call(
+    grad_q, kgr, vgr, back, pay, send = pl.pallas_call(
         functools.partial(front_kernel, groups, per_group),
         grid=(skip,),
         in_specs=query_specs(0)
@@ -649,6 +671,7 @@
             whole((WINDOW, width)),
             whole((WINDOW, 2 * width)),
             whole((pay_rows, LANES)),
+            whole((pay_rows, LANES)),
         ],
         out_shape=[
             full_q,
@@ -656,6 +679,7 @@
             full_k,
             jax.ShapeDtypeStruct((WINDOW, 2 * width), bf16),
             pay_f,
+            jax.ShapeDtypeStruct((pay_rows, LANES), bf16),
         ],
         input_output_aliases={14: 0, 15: 1, 16: 2},
         scratch_shapes=scratch(2 * WINDOW),
@@ -663,7 +687,7 @@
         name="front",
     )(*query_args, *key_args, rot, halo, front, part, grad_q, kgr, vgr)
 
-    pays = addends(pay, "seq")
+    pays = addends(pay, "seq", send, functools.partial(packed, width // 2))
     back = lax.ppermute(back, "seq", backward)
     kgr, vgr = pl.pallas_call(
         keys_kernel,
@@ -682,6 +706,7 @@
         cost_estimate=pl.CostEstimate(
             flops=1_000_000_000, bytes_accessed=3_000_000, transcendentals=0
         ),
+        compiler_params=pltpu.CompilerParams(vmem_limit_bytes=8 * 1024 * 1024),
         name="keys",
     )(tail, back, key_words, rot, kgr, vgr)
     raw, square, sink_sum = pl.pallas_call(
@@ -691,11 +716,13 @@
             jax.ShapeDtypeStruct((8, LANES), f32),
             jax.ShapeDtypeStruct((1, sinks.shape[0]), f32),
         ],
+        compiler_params=pltpu.CompilerParams(vmem_limit_bytes=8 * 1024 * 1024),
         name="raw",
     )(rotation, *pays)
     grad_rotation = pl.pallas_call(
         functools.partial(scale_kernel, limit_value),
         out_shape=jax.ShapeDtypeStruct((groups, head, head), f32),
+        compiler_params=pltpu.CompilerParams(vmem_limit_bytes=8 * 1024 * 1024),
         name="scale",
     )(raw, *addends(square, "head"))
     return (
@@ -709,7 +736,7 @@
 
 def solution(mesh):
     return jax.shard_map(
-        per_device,
+        device_work,
         mesh=mesh,
         in_specs=(
             P("seq", "head"),

time: 75.2 us -> 63.7 us (0.85)
  local copies, waits for them, and re-layouts: 14.8 us -> 3.6 us
  Pallas kernels: 35.6 us -> 34.2 us
  other arithmetic: 0.02 us -> 1.01 us
    unnamed x36 -> x8, local copies, waits for them, and re-layouts: 14.8 us -> 3.6 us
    pallas_call x6, Pallas kernels: 35.6 us -> 34.2 us  [the longest x1 24.1 us: device_work(): pl.pallas_call(functools.partial(main_kernel, groups, per_group), grid=(r...]
    sub x0 -> x1, other arithmetic: none -> 0.91 us  [packed(): rest = x - lax.reduce_precision(x, 8, 7)]
  transfers between devices with their start and end apart: 9 -> 9, of which waited for: 5 -> 5; matrix products, arithmetic and copies ran while one was open for 0% -> 2% of each run, Pallas kernels for 37% -> 41%
where the time goes in v3:
time: 63.7 us; the launch traced here: 63.3 us
  Pallas kernels  34.2 us (54%)
  starting transfers between devices  14.8 us (23%)
  waiting for transfers between devices  9.02 us (14%)
  local copies, waits for them, and re-layouts  3.6 us (6%)
  other arithmetic  1.01 us (2%)
  between operations  0.69 us (1%)
    pallas_call x1, Pallas kernels, device_work(): pl.pallas_call(functools.partial(main_kernel, groups, per_group), grid=(r...  24.1 us
    ppermute x7, waiting for transfers between devices, addends(): parts.append(lax.ppermute(out, axis, swap))  9.01 us
    ppermute x7, starting transfers between devices, addends(): parts.append(lax.ppermute(out, axis, swap))  8.01 us
    pallas_call x1, Pallas kernels, device_work(): pl.pallas_call(functools.partial(front_kernel, groups, per_group), grid=(...  5.56 us
    ppermute x1, starting transfers between devices, device_work(): halo = lax.ppermute(halo, 'seq', forward)  5.53 us
    unnamed x8, local copies, waits for them, and re-layouts  3.6 us
    pallas_call x1, Pallas kernels, device_work(): pl.pallas_call(halo_kernel, grid=(1,), in_specs=key_specs(WINDOW, last),...  1.83 us
    ppermute x1, starting transfers between devices, device_work(): back = lax.ppermute(back, 'seq', backward)  1.28 us
  transfers between devices with their start and end apart: 9, of which 5 were waited for; matrix products, arithmetic and copies ran while one was open for 2% of the time, Pallas kernels for 41%

profile of v3, /device:TPU:0, one launch (start us, length us, event | category | flops | bytes accessed | tf_op | source)
XLA Modules:
  0.0 63.3 jit_solution(13121370435498615878)
XLA Ops:
  0.6 1.8 %halo.1 = bf16[128,640]{1,0:T(8,128)(2,1)} custom-call(bf16[1024,256]{1,0:T(8,128)(2,1)} %k_ref.5, s32[8,1024]{1,0:T(8,128)} %bitcast.13, bf16[1024,256]{1,0:T(8,128)(2,1)} %v_ref.5, s32[8,1024]{1,0:T(8,128)} %bitcast.16, s32[16,1024]{1,0:T(8,128)} %bitcast.6), custom_call_target="tpu_custom_call" | custom-call | tf_op jit(solution)/shard_map/halo/pallas_call | solution.py:588
  2.5 5.5 %collective-permute-start = (bf16[128,640]{1,0:T(8,128)(2,1)}, bf16[128,640]{1,0:T(8,128)(2,1)}, u32[]{:S(2)}, u32[]{:S(2)}) collective-permute-start(bf16[128,640]{1,0:T(8,128)(2,1)} %halo.1), channel_id=1, source_target_pairs={{0,2},{2,4},{4,6},{6,8},{8,10},{10,12},{12,14},{14,16},{16,18},{18... | collective-permute-start | bytes 491528 | tf_op jit(solution)/shard_map/ppermute | solution.py:596
  8.0 24.1 %attend.1 = (bf16[1024,2048]{1,0:T(8,128)(2,1)}, bf16[1024,256]{1,0:T(8,128)(2,1)}, bf16[1024,256]{1,0:T(8,128)(2,1)}, f32[128,512]{1,0:T(8,128)}, f32[128,512]{1,0:T(8,128)}, /*index=5*/f32[144,128]{1,0:T(8,128)}) custom-call(f32[32]{0:T(128)} %sink_ref.3, bf16[1024,2048]{1,0:T(8,128)(2,1)} %q_ref.3, s32[64,1024]{1,0:T(8,128)} %bitcast.11, ...), custom_call_target="tpu_custom_call" | custom-call | flops 60000002048 | bytes 60000000 | tf_op jit(solution)/shard_map/attend/pallas_call | solution.py:632
  32.1 0.0 collective-permute-done.halo_ref
  32.1 5.6 %front.1 = (bf16[1024,2048]{1,0:T(8,128)(2,1)}, bf16[1024,256]{1,0:T(8,128)(2,1)}, bf16[1024,256]{1,0:T(8,128)(2,1)}, bf16[128,512]{1,0:T(8,128)(2,1)}, f32[144,128]{1,0:T(8,128)}, /*index=5*/bf16[144,128]{1,0:T(8,128)(2,1)}) custom-call(f32[32]{0:T(128)} %sink_ref.3, ...), custom_call_target="tpu_custom_call", output_to_operand_aliasing={{0}: (14, {}), {1}: (15, {}), {2}: (16, {})} | custom-call | tf_op jit(solution)/shard_map/front/pallas_call | solution.py:654
  37.7 0.9 %collective-permute-start.2 = (bf16[144,128]{1,0:T(8,128)(2,1)}, bf16[144,128]{1,0:T(8,128)(2,1)S(1)}, u32[]{:S(2)}, u32[]{:S(2)}) collective-permute-start(bf16[144,128]{1,0:T(8,128)(2,1)} %get-tuple-element.35), channel_id=1, source_target_pairs={{0,2},{2,0},{4,6},{6,4},{8,10},{10,8},{12,14},{14,12},{16,18},{18,... | collective-permute-start | bytes 110600 | tf_op jit(solution)/shard_map/ppermute | solution.py:521
  38.6 1.5 %collective-permute-start.3 = (bf16[144,128]{1,0:T(8,128)(2,1)}, bf16[144,128]{1,0:T(8,128)(2,1)S(1)}, u32[]{:S(2)}, u32[]{:S(2)}) collective-permute-start(bf16[144,128]{1,0:T(8,128)(2,1)} %get-tuple-element.35), channel_id=1, source_target_pairs={{0,4},{2,6},{4,0},{6,2},{8,12},{10,14},{12,8},{14,10},{16,20},{18,... | collective-permute-start | bytes 110600 | tf_op jit(solution)/shard_map/ppermute | solution.py:521
  40.1 1.1 %collective-permute-start.4 = (bf16[144,128]{1,0:T(8,128)(2,1)}, bf16[144,128]{1,0:T(8,128)(2,1)S(1)}, u32[]{:S(2)}, u32[]{:S(2)}) collective-permute-start(bf16[144,128]{1,0:T(8,128)(2,1)} %get-tuple-element.35), channel_id=1, source_target_pairs={{0,6},{2,4},{4,2},{6,0},{8,14},{10,12},{12,10},{14,8},{16,22},{18,... | collective-permute-start | bytes 110600 | tf_op jit(solution)/shard_map/ppermute | solution.py:521
  41.2 1.3 %collective-permute-start.1 = (bf16[128,512]{1,0:T(8,128)(2,1)}, bf16[128,512]{1,0:T(8,128)(2,1)S(1)}, u32[]{:S(2)}, u32[]{:S(2)}) collective-permute-start(bf16[128,512]{1,0:T(8,128)(2,1)} %get-tuple-element.29), channel_id=1, source_target_pairs={{2,0},{4,2},{6,4},{8,6},{10,8},{12,10},{14,12},{16,14},{18,16},{20... | collective-permute-start | bytes 393224 | tf_op jit(solution)/shard_map/ppermute | solution.py:691
  42.5 0.0 collective-permute-done.2
  42.5 0.2 collective-permute-done.3
  42.8 2.7 %collective-permute-done.4 = bf16[144,128]{1,0:T(8,128)(2,1)S(1)} collective-permute-done((bf16[144,128]{1,0:T(8,128)(2,1)}, bf16[144,128]{1,0:T(8,128)(2,1)S(1)}, u32[]{:S(2)}, u32[]{:S(2)}) %collective-permute-start.4) | collective-permute-done | bytes 36896 | tf_op jit(solution)/shard_map/ppermute | solution.py:521
  45.4 0.9 %reduce-precision_subtract_fusion = (f32[144,128]{1,0:T(8,128)S(1)}, f32[144,128]{1,0:T(8,128)S(1)}) fusion(bf16[144,128]{1,0:T(8,128)(2,1)S(1)} %collective-permute-done.4, bf16[144,128]{1,0:T(8,128)(2,1)S(1)} %collective-permute-done.3, f32[144,128]{1,0:T(8,128)} %get-tuple-element.34, bf16[144,128]{1,0:T(8,128)(2,1)S(1)} %collective-permute-done.2), kind=kLoop, calls=%fused_computation.1 | loop fusion | flops 147456 | bytes 331776 | tf_op jit(solution)/shard_map/sub | solution.py:527
  46.4 0.1 fusion
  46.5 1.6 %collective-permute-start.5 = (bf16[144,128]{1,0:T(8,128)(2,1)S(1)}, bf16[144,128]{1,0:T(8,128)(2,1)S(1)}, u32[]{:S(2)}, u32[]{:S(2)}) collective-permute-start(bf16[144,128]{1,0:T(8,128)(2,1)S(1)} %fusion), channel_id=1, source_target_pairs={{0,8},{2,10},{4,12},{6,14},{8,0},{10,2},{12,4},{14,6},{16,24},{18,... | collective-permute-start | bytes 110600 | tf_op jit(solution)/shard_map/ppermute | solution.py:521
  48.1 2.0 %collective-permute-start.6 = (bf16[144,128]{1,0:T(8,128)(2,1)S(1)}, bf16[144,128]{1,0:T(8,128)(2,1)S(1)}, u32[]{:S(2)}, u32[]{:S(2)}) collective-permute-start(bf16[144,128]{1,0:T(8,128)(2,1)S(1)} %fusion), channel_id=1, source_target_pairs={{0,16},{2,18},{4,20},{6,22},{8,24},{10,26},{12,28},{14,30},{16,0},... | collective-permute-start | bytes 110600 | tf_op jit(solution)/shard_map/ppermute | solution.py:521
  50.1 0.8 %collective-permute-start.7 = (bf16[144,128]{1,0:T(8,128)(2,1)S(1)}, bf16[144,128]{1,0:T(8,128)(2,1)S(1)}, u32[]{:S(2)}, u32[]{:S(2)}) collective-permute-start(bf16[144,128]{1,0:T(8,128)(2,1)S(1)} %fusion), channel_id=1, source_target_pairs={{0,24},{2,26},{4,28},{6,30},{8,16},{10,18},{12,20},{14,22},{16,8},... | collective-permute-start | bytes 110600 | tf_op jit(solution)/shard_map/ppermute | solution.py:521
  50.9 0.0 collective-permute-done.5.refs_1_
  50.9 2.7 %collective-permute-done.6.refs_2_ = bf16[144,128]{1,0:T(8,128)(2,1)S(1)} collective-permute-done((bf16[144,128]{1,0:T(8,128)(2,1)S(1)}, bf16[144,128]{1,0:T(8,128)(2,1)S(1)}, u32[]{:S(2)}, u32[]{:S(2)}) %collective-permute-start.6) | collective-permute-done | bytes 36896 | tf_op jit(solution)/shard_map/ppermute | solution.py:521
  53.6 2.2 %collective-permute-done.7.refs_3_ = bf16[144,128]{1,0:T(8,128)(2,1)S(1)} collective-permute-done((bf16[144,128]{1,0:T(8,128)(2,1)S(1)}, bf16[144,128]{1,0:T(8,128)(2,1)S(1)}, u32[]{:S(2)}, u32[]{:S(2)}) %collective-permute-start.7) | collective-permute-done | bytes 36896 | tf_op jit(solution)/shard_map/ppermute | solution.py:521
  55.9 0.0 copy-start
  55.9 0.9 %copy-done = f32[4,64,64]{2,1,0:T(8,128)S(1)} copy-done((f32[4,64,64]{2,1,0:T(8,128)S(1)}, f32[4,64,64]{2,1,0:T(8,128)}, u32[]{:S(2)}) %copy-start) | copy-done | bytes 65560
  56.8 0.8 %raw.1 = (f32[4,64,64]{2,1,0:T(8,128)S(1)}, f32[8,128]{1,0:T(8,128)S(1)}, f32[1,32]{1,0:T(1,128)}) custom-call(f32[4,64,64]{2,1,0:T(8,128)S(1)} %copy-done, f32[144,128]{1,0:T(8,128)S(1)} %get-tuple-element.40.refs_0_, bf16[144,128]{1,0:T(8,128)(2,1)S(1)} %collective-permute-done.5.refs_1_, bf16[144,128]{1,0:T(8,128)(2,1)S(1)} %collective-permute-done.6.refs_2_, ...), custom_call_target="tpu_custom_call" | custom-call | tf_op jit(solution)/shard_map/raw/pallas_call | solution.py:712
  57.6 0.0 collective-permute-start.8
  57.6 1.2 %collective-permute-done.8.refs_1_ = f32[8,128]{1,0:T(8,128)S(1)} collective-permute-done((f32[8,128]{1,0:T(8,128)S(1)}, f32[8,128]{1,0:T(8,128)S(1)}, u32[]{:S(2)}, u32[]{:S(2)}) %collective-permute-start.8) | collective-permute-done | bytes 4128 | tf_op jit(solution)/shard_map/ppermute | solution.py:521
  58.8 0.7 %scale.1 = f32[4,64,64]{2,1,0:T(8,128)} custom-call(f32[4,64,64]{2,1,0:T(8,128)S(1)} %get-tuple-element.36.raw_ref, f32[8,128]{1,0:T(8,128)S(1)} %get-tuple-element.37.refs_0_, f32[8,128]{1,0:T(8,128)S(1)} %collective-permute-done.8.refs_1_), custom_call_target="tpu_custom_call" | custom-call | tf_op jit(solution)/shard_map/scale/pallas_call | solution.py:722
  59.5 0.0 collective-permute-done.1.back_ref
  59.5 0.0 copy-start.1
  59.5 0.9 %copy-done.1 = f32[4,64,64]{2,1,0:T(8,128)S(1)} copy-done((f32[4,64,64]{2,1,0:T(8,128)S(1)}, f32[4,64,64]{2,1,0:T(8,128)}, u32[]{:S(2)}) %copy-start.1) | copy-done | bytes 65560
  60.4 0.0 copy-start.2
  60.4 0.8 %copy-done.2 = s32[1024,16]{0,1:T(8,128)S(1)} copy-done((s32[1024,16]{0,1:T(8,128)S(1)}, s32[1024,16]{0,1:T(8,128)}, u32[]{:S(2)}) %copy-start.2) | copy-done | bytes 65560
  61.3 0.0 copy-start.3
  61.3 0.9 %copy-done.3 = f32[128,512]{1,0:T(8,128)S(1)} copy-done((f32[128,512]{1,0:T(8,128)S(1)}, f32[128,512]{1,0:T(8,128)}, u32[]{:S(2)}) %copy-start.3) | copy-done | bytes 262168
  62.2 1.1 %keys.1 = (bf16[1024,256]{1,0:T(8,128)(2,1)}, bf16[1024,256]{1,0:T(8,128)(2,1)}) custom-call(f32[128,512]{1,0:T(8,128)S(1)} %copy-done.3, bf16[128,512]{1,0:T(8,128)(2,1)S(1)} %collective-permute-done.1.back_ref, s32[16,1024]{1,0:T(8,128)S(1)} %bitcast.9, f32[4,64,64]{2,1,0:T(8,128)S(1)} %copy-done.1, ...), custom_call_target="tpu_custom_call", output_to_operand_aliasing={{0}: (4, {}), {1}: (5, {})} | custom-call | flops 1000000000 | bytes 3000000 | tf_op jit(solution)/shard_map/keys/pallas_call | solution.py:692
  (2 shorter events, 0.0 us)
Async XLA Ops:
  2.5 29.7 %collective-permute-start = (bf16[128,640]{1,0:T(8,128)(2,1)}, bf16[128,640]{1,0:T(8,128)(2,1)}, u32[]{:S(2)}, u32[]{:S(2)}) collective-permute-start(bf16[128,640]{1,0:T(8,128)(2,1)} %halo.1), channel_id=1, source_target_pairs={{0,2},{2,4},{4,6},{6,8},{8,10},{10,12},{12,14},{14,16},{16,18},{18... | collective-permute-start | bytes 491528 | tf_op jit(solution)/shard_map/ppermute | solution.py:596
  37.7 4.9 %collective-permute-start.2 = (bf16[144,128]{1,0:T(8,128)(2,1)}, bf16[144,128]{1,0:T(8,128)(2,1)S(1)}, u32[]{:S(2)}, u32[]{:S(2)}) collective-permute-start(bf16[144,128]{1,0:T(8,128)(2,1)} %get-tuple-element.35), channel_id=1, source_target_pairs={{0,2},{2,0},{4,6},{6,4},{8,10},{10,8},{12,14},{14,12},{16,18},{18,... | collective-permute-start | bytes 110600 | tf_op jit(solution)/shard_map/ppermute | solution.py:521
  38.6 4.2 %collective-permute-start.3 = (bf16[144,128]{1,0:T(8,128)(2,1)}, bf16[144,128]{1,0:T(8,128)(2,1)S(1)}, u32[]{:S(2)}, u32[]{:S(2)}) collective-permute-start(bf16[144,128]{1,0:T(8,128)(2,1)} %get-tuple-element.35), channel_id=1, source_target_pairs={{0,4},{2,6},{4,0},{6,2},{8,12},{10,14},{12,8},{14,10},{16,20},{18,... | collective-permute-start | bytes 110600 | tf_op jit(solution)/shard_map/ppermute | solution.py:521
  40.1 5.3 %collective-permute-start.4 = (bf16[144,128]{1,0:T(8,128)(2,1)}, bf16[144,128]{1,0:T(8,128)(2,1)S(1)}, u32[]{:S(2)}, u32[]{:S(2)}) collective-permute-start(bf16[144,128]{1,0:T(8,128)(2,1)} %get-tuple-element.35), channel_id=1, source_target_pairs={{0,6},{2,4},{4,2},{6,0},{8,14},{10,12},{12,10},{14,8},{16,22},{18,... | collective-permute-start | bytes 110600 | tf_op jit(solution)/shard_map/ppermute | solution.py:521
  41.2 18.3 %collective-permute-start.1 = (bf16[128,512]{1,0:T(8,128)(2,1)}, bf16[128,512]{1,0:T(8,128)(2,1)S(1)}, u32[]{:S(2)}, u32[]{:S(2)}) collective-permute-start(bf16[128,512]{1,0:T(8,128)(2,1)} %get-tuple-element.29), channel_id=1, source_target_pairs={{2,0},{4,2},{6,4},{8,6},{10,8},{12,10},{14,12},{16,14},{18,16},{20... | collective-permute-start | bytes 393224 | tf_op jit(solution)/shard_map/ppermute | solution.py:691
  46.5 4.5 %collective-permute-start.5 = (bf16[144,128]{1,0:T(8,128)(2,1)S(1)}, bf16[144,128]{1,0:T(8,128)(2,1)S(1)}, u32[]{:S(2)}, u32[]{:S(2)}) collective-permute-start(bf16[144,128]{1,0:T(8,128)(2,1)S(1)} %fusion), channel_id=1, source_target_pairs={{0,8},{2,10},{4,12},{6,14},{8,0},{10,2},{12,4},{14,6},{16,24},{18,... | collective-permute-start | bytes 110600 | tf_op jit(solution)/shard_map/ppermute | solution.py:521
  48.1 5.5 %collective-permute-start.6 = (bf16[144,128]{1,0:T(8,128)(2,1)S(1)}, bf16[144,128]{1,0:T(8,128)(2,1)S(1)}, u32[]{:S(2)}, u32[]{:S(2)}) collective-permute-start(bf16[144,128]{1,0:T(8,128)(2,1)S(1)} %fusion), channel_id=1, source_target_pairs={{0,16},{2,18},{4,20},{6,22},{8,24},{10,26},{12,28},{14,30},{16,0},... | collective-permute-start | bytes 110600 | tf_op jit(solution)/shard_map/ppermute | solution.py:521
  50.1 5.8 %collective-permute-start.7 = (bf16[144,128]{1,0:T(8,128)(2,1)S(1)}, bf16[144,128]{1,0:T(8,128)(2,1)S(1)}, u32[]{:S(2)}, u32[]{:S(2)}) collective-permute-start(bf16[144,128]{1,0:T(8,128)(2,1)S(1)} %fusion), channel_id=1, source_target_pairs={{0,24},{2,26},{4,28},{6,30},{8,16},{10,18},{12,20},{14,22},{16,8},... | collective-permute-start | bytes 110600 | tf_op jit(solution)/shard_map/ppermute | solution.py:521
  55.9 0.9 %copy-start = (f32[4,64,64]{2,1,0:T(8,128)S(1)}, f32[4,64,64]{2,1,0:T(8,128)}, u32[]{:S(2)}) copy-start(f32[4,64,64]{2,1,0:T(8,128)} %rot_ref.7) | copy-start | bytes 196612
  57.6 1.2 %collective-permute-start.8 = (f32[8,128]{1,0:T(8,128)S(1)}, f32[8,128]{1,0:T(8,128)S(1)}, u32[]{:S(2)}, u32[]{:S(2)}) collective-permute-start(f32[8,128]{1,0:T(8,128)S(1)} %get-tuple-element.37.refs_0_), channel_id=1, source_target_pairs={{0,1},{1,0},{2,3},{3,2},{4,5},{5,4},{6,7},{7,6},{8,9},{9,8},{10,11... | collective-permute-start | bytes 12296 | tf_op jit(solution)/shard_map/ppermute | solution.py:521
  59.5 0.9 %copy-start.1 = (f32[4,64,64]{2,1,0:T(8,128)S(1)}, f32[4,64,64]{2,1,0:T(8,128)}, u32[]{:S(2)}) copy-start(f32[4,64,64]{2,1,0:T(8,128)} %rot_ref.7) | copy-start | bytes 196612
  60.4 0.8 %copy-start.2 = (s32[1024,16]{0,1:T(8,128)S(1)}, s32[1024,16]{0,1:T(8,128)}, u32[]{:S(2)}) copy-start(s32[1024,16]{0,1:T(8,128)} %param.18) | copy-start | bytes 196612
  61.3 0.9 %copy-start.3 = (f32[128,512]{1,0:T(8,128)S(1)}, f32[128,512]{1,0:T(8,128)}, u32[]{:S(2)}) copy-start(f32[128,512]{1,0:T(8,128)} %get-tuple-element.28.tail_ref) | copy-start | bytes 786436

commit v4 on v3

--- a/solution.py
+++ b/solution.py
@@ -65,24 +65,22 @@
     return (mm_tn(first, low) + mm_tn(second, high)).astype(bf16)
 
 
-def byte_flags(byte_rows, width):
-    count = width // WORD_BITS
-    shape = (LANES, width)
-    lane, row = iota(shape, 1), iota(shape, 0)
-    upper = (lane % WORD_BITS) // 8
-    spread = zero_one(row == lane // WORD_BITS + upper * count)
-    value = mm(byte_rows, spread).astype(i32)
-    bit = jnp.left_shift(jnp.ones((1, width), i32), iota((1, width), 1) % 8)
-    return (value & bit) != 0
-
-
-def turn_pair(rot_ref, pair):
-    first = rot_ref[2 * pair].astype(bf16)
-    zero = jnp.zeros_like(first)
-    second = rot_ref[2 * pair + 1].astype(bf16)
-    return jnp.concatenate(
-        [jnp.concatenate([first, zero], axis=1), jnp.concatenate([zero, second], axis=1)], axis=0
+def entry_flags(words):
+    count, rows = words.shape
+    spots = jnp.concatenate(
+        [jnp.broadcast_to(words[n : n + 1], (WORD_BITS, rows)) for n in range(count)], axis=0
     )
+    row = iota((count * WORD_BITS, 1), 0)
+    return (spots & jnp.left_shift(jnp.ones_like(row), row % WORD_BITS)) != 0
+
+
+def raw_keys(masked, rot_ref):
+    head = rot_ref.shape[1]
+    turned = [
+        mm(rot_ref[g].astype(bf16), masked[g * head : (g + 1) * head])
+        for g in range(masked.shape[0] // head)
+    ]
+    return jnp.transpose(jnp.concatenate(turned, axis=0).astype(bf16))
 
 
 def halo_kernel(k_ref, ke_ref, v_ref, ve_ref, w_ref, out_ref):
@@ -106,7 +104,6 @@
     column = iota((UNIT, lanes), 1) % UNIT
     current = iota((UNIT, lanes), 0) <= column
     low = zero_one(iota((UNIT, lanes), 0) > column)
-    lower = iota((1, LANES), 1) < head
     bit = jnp.left_shift(jnp.ones((head, 1), i32), iota((head, 1), 0) % WORD_BITS)
     per_pair = 2 * head // WORD_BITS
     per_scale = 2 * head // SHARED_EXPONENT
@@ -153,13 +150,6 @@
             shared[g, s] = (qt, turned_tile(do_ref, g, s))
         return shared[g, s]
 
-    def pair_operands(g, s):
-        other = g + 1 if g % 2 == 0 else g - 1
-        mine = operands(g, s)
-        theirs = operands(other, s) if other < groups else mine
-        first, second = (mine, theirs) if g % 2 == 0 else (theirs, mine)
-        return [jnp.concatenate([x, y], axis=0) for x, y in zip(first, second)]
-
     def band(s):
         return pl.ds(start + s * UNIT, BAND)
 
@@ -179,14 +169,15 @@
         spots = side_by_side(words, g * side * per_pair, per_pair, s)
         return kg[g, band(s), :], vg[g, band(s), :], sinks[pl.ds(g, 1), :], spots
 
-    def products(g, s, loaded):
-        keys, values, _, _ = loaded
-        qt, dt = operands(g, s)
-        scores = mm(keys, qt)
+    def scores_of(g, s, loaded):
+        scores = mm(loaded[0], operands(g, s)[0])
         if edge:
             limit = jnp.where(lax.axis_index("seq") == 0, WINDOW, 0) - (start + s * UNIT)
             scores = jnp.where(iota((BAND, 1), 0) >= limit, scores, negative)
-        return combined(scores), combined(mm(values, dt))
+        return combined(scores)
+
+    def gprobs_of(g, s, loaded):
+        return combined(mm(loaded[1], operands(g, s)[1]))
 
     def soft(g, s, loaded, scores, gprobs):
         sink = loaded[2]
@@ -200,10 +191,20 @@
         term = sink_numer * inverse * delta
         return spread(weights.astype(bf16)), spread(gscores), term
 
-    def gradients(g, s, probs, grads):
-        ktr = shared["k", g // 2, s][(g % 2) * head : (g % 2 + 1) * head]
-        both_q, both_d = pair_operands(g, s)
-        return mm(ktr, grads), mm_nt(grads, both_q), mm_nt(probs, both_d)
+    def grad_query(g, s, grads):
+        return mm(shared["k", g // 2, s][(g % 2) * head : (g % 2 + 1) * head], grads)
+
+    def grad_keys(g, s, grads):
+        return in_window(mm_nt(operands(g, s)[0], grads), s)
+
+    def grad_values(g, s, probs):
+        return in_window(mm_nt(operands(g, s)[1], probs), s)
+
+    def in_window(x, s):
+        before, after = s * UNIT, STEP - UNIT - s * UNIT
+        zeros = [jnp.zeros((head, n), f32) for n in (before, after)]
+        parts = [zeros[0]] * (before > 0) + [x] + [zeros[1]] * (after > 0)
+        return jnp.concatenate(parts, axis=1)
 
     def clipped(g, s, loaded, dq):
         spots = loaded[3]
@@ -223,10 +224,14 @@
             ],
             axis=1,
         )
-        masked = jnp.where((spots & bit) != 0, dq, 0.0).astype(bf16)
+        return jnp.where((spots & bit) != 0, dq, 0.0).astype(bf16)
+
+    def turned_back(g, s, masked):
         turned = mm(rot_ref[g].astype(bf16), masked).astype(bf16)
-        turned = jnp.concatenate([turned[:, :half_lanes], turned[:, half_lanes:]], axis=0)
-        return mm_nt(masked, pair_operands(g, s)[0]), turned
+        return jnp.concatenate([turned[:, :half_lanes], turned[:, half_lanes:]], axis=0)
+
+    def rotation_term(g, s, masked):
+        return mm_nt(masked, operands(g, s)[0])
 
     sums = {}
 
@@ -238,16 +243,16 @@
                 p * UNIT : (p + 1) * UNIT
             ]
         accs[pl.ds(g, 1), :] -= term
-        sums[g, s] = parts
-        if g % 2 == 0 and g + 1 < groups:
+        if s:
+            parts = tuple(x + y for x, y in zip(sums[g], parts))
+        sums[g] = parts
+        if s + 1 < STEP // UNIT:
             return
-        pair = g // 2
-        at = pair * LANES
-        left = sums[2 * pair, s]
-        right = parts if g % 2 else (0.0, 0.0, 0.0)
-        acck[band(s), at : at + LANES] += jnp.where(lower, left[0], right[0])
-        accv[band(s), at : at + LANES] += jnp.where(lower, left[1], right[1])
-        accp[pair * head : (pair + 1) * head] += jnp.where(lower, left[2], right[2])
+        window = pl.ds(start, WINDOW + STEP)
+        mine = slice(g * head, (g + 1) * head)
+        acck[mine, window] += parts[0]
+        accv[mine, window] += parts[1]
+        accp[mine] += parts[2]
 
     units = [
         (g, s)
@@ -256,27 +261,36 @@
         for g in (2 * pair, 2 * pair + 1)
         if g < groups
     ]
-    loaded, ready, rounded, part, done = {}, {}, {}, {}, {}
+    loaded, scores, gprobs, soft_out, masked, turned = ({} for _ in range(6))
+    dk, dv, dp = {}, {}, {}
+    wide = 2
+    teams = [range(n, min(n + wide, len(units))) for n in range(0, len(units), wide)]
 
     def stage(n, lead):
         n += lead
-        return n if 0 <= n < len(units) else None
-
-    for turn in range(-AHEAD, len(units) + LAG):
-        if (n := stage(turn, AHEAD)) is not None:
+        return teams[n] if 0 <= n < len(teams) else ()
+
+    for turn in range(-AHEAD, len(teams) + LAG):
+        for n in stage(turn, AHEAD):
             loaded[n] = fetch(*units[n])
-        if (n := stage(turn, 1)) is not None:
-            ready[n] = products(*units[n], loaded[n])
-        if (n := stage(turn, 0)) is not None:
-            rounded[n] = soft(*units[n], loaded[n], *ready.pop(n))
-        if (n := stage(turn, -1)) is not None:
-            part[n] = gradients(*units[n], *rounded[n][:2])
-        if (n := stage(turn, -2)) is not None:
-            dq, dk, dv = part.pop(n)
-            dp, turned = clipped(*units[n], loaded[n], dq)
-            done[n] = (rounded[n][2], turned, dk, dv, dp)
-        if (n := stage(turn, -LAG)) is not None:
-            finish(*units[n], *done.pop(n))
+        for n in stage(turn, -1):
+            masked[n] = clipped(*units[n], loaded[n], grad_query(*units[n], soft_out[n][1]))
+        for n in stage(turn, 1):
+            scores[n] = scores_of(*units[n], loaded[n])
+        for n in stage(turn, -1):
+            dk[n] = grad_keys(*units[n], soft_out[n][1])
+        for n in stage(turn, 1):
+            gprobs[n] = gprobs_of(*units[n], loaded[n])
+        for n in stage(turn, -1):
+            dv[n] = grad_values(*units[n], soft_out[n][0])
+        for n in stage(turn, -2):
+            turned[n] = turned_back(*units[n], masked[n])
+        for n in stage(turn, -2):
+            dp[n] = rotation_term(*units[n], masked[n])
+        for n in stage(turn, 0):
+            soft_out[n] = soft(*units[n], loaded[n], scores.pop(n), gprobs.pop(n))
+        for n in stage(turn, -LAG):
+            finish(*units[n], soft_out[n][2], turned[n], dk[n], dv[n], dp[n])
 
 
 def prepare(groups, per_group, sink_ref, keys, values, scratch):
@@ -313,13 +327,20 @@
     return jnp.sum(total, axis=0, keepdims=True)
 
 
-def key_terms(gk, flags, kn_rows, pair):
-    at = pair * LANES
-    head = LANES // 2
-    masked = jnp.where(flags[:, at : at + LANES], gk[:, at : at + LANES], 0.0).astype(bf16)
-    both = mm_tn(masked, kn_rows[:, at : at + LANES]) * float(head) ** 0.5
-    lower = iota((1, LANES), 1) < head
-    return masked, jnp.where(lower, both[:head], both[head:])
+def with_keys(gk, words, rows, scratch, pay_ref):
+    _, kg, _, _, _, accp, _, _ = scratch
+    head = kg.shape[2]
+    masked = jnp.where(entry_flags(words), gk, 0.0).astype(bf16)
+    for pair in range(gk.shape[0] // LANES):
+        sums = []
+        for g in (2 * pair, 2 * pair + 1):
+            mine = slice(g * head, (g + 1) * head)
+            total = accp[mine]
+            if g < kg.shape[0]:
+                total = total + mm(masked[mine], kg[g, rows, :]) * float(head) ** 0.5
+            sums.append(total)
+        pay_ref[pair * head : (pair + 1) * head] = jnp.concatenate(sums, axis=1)
+    return masked
 
 
 def main_kernel(
@@ -344,7 +365,7 @@
     pay_ref,
     *scratch,
 ):
-    kn, _, _, acck, accv, accp, accs, _ = scratch
+    _, _, _, acck, accv, accp, accs, _ = scratch
     b = pl.program_id(0)
     rows, width = k_ref.shape
     head = LANES // 2
@@ -363,22 +384,16 @@
 
     @pl.when(b == pl.num_programs(0) - 1)
     def _():
-        scale = head**-0.5
-        front_ref[:, :width] = acck[:WINDOW]
-        front_ref[:, width:] = accv[:WINDOW]
-        gk = acck[WINDOW:] * scale
-        gv = accv[WINDOW:]
-        tail_ref[:, :width] = gk[rows - 2 * WINDOW :]
-        tail_ref[:, width:] = gv[rows - 2 * WINDOW :]
-        vgr_ref[WINDOW:] = gv.astype(bf16)
-        flags = byte_flags(word_bytes(kw_ref[...])[WINDOW:], width)
-        for pair in range(width // LANES):
-            at = pair * LANES
-            masked, term = key_terms(gk, flags, kn[WINDOW:], pair)
-            kgr_ref[WINDOW:, at : at + LANES] = mm_nt(masked, turn_pair(rot_ref, pair)).astype(bf16)
-            pay_ref[pair * head : (pair + 1) * head] = (
-                accp[pair * head : (pair + 1) * head] + term
-            )
+        front_ref[:width] = acck[:, :WINDOW]
+        front_ref[width:] = accv[:, :WINDOW]
+        gk = acck[:, WINDOW:] * (head**-0.5)
+        gv = accv[:, WINDOW:]
+        tail_ref[:width] = gk[:, rows - 2 * WINDOW :]
+        tail_ref[width : 2 * width] = gv[:, rows - 2 * WINDOW :]
+        tail_ref[2 * width :] = kw_ref[:, rows - WINDOW :].astype(f32)
+        vgr_ref[WINDOW:] = jnp.transpose(gv.astype(bf16))
+        masked = with_keys(gk, kw_ref[:, WINDOW:], pl.ds(WINDOW, rows - WINDOW), scratch, pay_ref)
+        kgr_ref[WINDOW:] = raw_keys(masked, rot_ref)
         pay_ref[width // 2 :] = jnp.broadcast_to(sink_sums(groups, per_group, accs), (16, LANES))
 
 
@@ -410,7 +425,7 @@
     send_ref,
     *scratch,
 ):
-    kn, _, _, acck, accv, accp, accs, _ = scratch
+    _, _, _, acck, accv, accp, accs, _ = scratch
     b = pl.program_id(0)
     width = k_ref.shape[1]
     head = LANES // 2
@@ -422,11 +437,14 @@
         keys = (halo_ref[:, :width], keys)
         values = (halo_ref[:, width : 2 * width], values)
         prepare(groups, per_group, sink_ref, keys, values, scratch)
-        acck[:WINDOW] = jnp.zeros((WINDOW, width), f32)
-        accv[:WINDOW] = jnp.zeros((WINDOW, width), f32)
-        acck[WINDOW:] = front_ref[:, :width]
-        accv[WINDOW:] = front_ref[:, width:]
-        accp[...] = part_ref[: width // 2]
+        acck[:, :WINDOW] = jnp.zeros((width, WINDOW), f32)
+        accv[:, :WINDOW] = jnp.zeros((width, WINDOW), f32)
+        acck[:, WINDOW:] = front_ref[:width]
+        accv[:, WINDOW:] = front_ref[width:]
+        for g in range(width // head):
+            accp[g * head : (g + 1) * head] = part_ref[
+                (g // 2) * head : (g // 2 + 1) * head, (g % 2) * head : (g % 2 + 1) * head
+            ]
 
     refs = (sink_ref, q_ref, qe_ref, do_ref, qw_ref, rot_ref, gq_ref)
     attend_step(groups, per_group, True, refs, scratch)
@@ -434,20 +452,16 @@
     @pl.when(b == pl.num_programs(0) - 1)
     def _():
         gk = acck[...] * (head**-0.5)
-        ret_ref[:, :width] = gk[:WINDOW].astype(bf16)
-        ret_ref[:, width:] = accv[:WINDOW].astype(bf16)
-        vgr_ref[...] = accv[WINDOW:].astype(bf16)
-        bytes_all = jnp.concatenate([halo_ref[:, 2 * width :], word_bytes(kw_ref[...])], axis=0)
-        flags = byte_flags(bytes_all, width)
-        for pair in range(width // LANES):
-            at = pair * LANES
-            masked, term = key_terms(gk, flags, kn[...], pair)
-            kgr_ref[:, at : at + LANES] = mm_nt(
-                masked[WINDOW:], turn_pair(rot_ref, pair)
-            ).astype(bf16)
-            pay_ref[pair * head : (pair + 1) * head] = (
-                accp[pair * head : (pair + 1) * head] + term
-            )
+        gv = accv[...].astype(bf16)
+        ret_ref[:width] = gk[:, :WINDOW].astype(bf16)
+        ret_ref[width:] = gv[:, :WINDOW]
+        vgr_ref[...] = jnp.transpose(gv[:, WINDOW:])
+        count = width // WORD_BITS
+        pieces = jnp.transpose(halo_ref[:, 2 * width :]).astype(f32)
+        words = (pieces[:count] + 256.0 * pieces[count : 2 * count]).astype(i32)
+        words = jnp.concatenate([words, kw_ref[...]], axis=1)
+        masked = with_keys(gk, words, slice(None), scratch, pay_ref)
+        kgr_ref[...] = raw_keys(masked[:, WINDOW:], rot_ref)
         sink = part_ref[width // 2 : width // 2 + 1] + sink_sums(groups, per_group, accs)
         tail_row = iota((16, LANES), 0)
         pay_ref[width // 2 :] = jnp.where(tail_row == 0, sink, 0.0)
@@ -458,17 +472,13 @@
         ).astype(bf16)
 
 
-def keys_kernel(tail_ref, back_ref, kw_ref, rot_ref, kgr_in, vgr_in, kgr_ref, vgr_ref):
+def keys_kernel(tail_ref, back_ref, rot_ref, kgr_in, vgr_in, kgr_ref, vgr_ref):
     width = kgr_ref.shape[1]
-    both = tail_ref[...] + back_ref[...].astype(f32)
-    flags = byte_flags(word_bytes(kw_ref[...]), width)
-    masked = jnp.where(flags, both[:, :width], 0.0).astype(bf16)
-    for pair in range(width // LANES):
-        at = pair * LANES
-        kgr_ref[:, at : at + LANES] = mm_nt(
-            masked[:, at : at + LANES], turn_pair(rot_ref, pair)
-        ).astype(bf16)
-    vgr_ref[...] = both[:, width:].astype(bf16)
+    both = tail_ref[: 2 * width] + back_ref[...].astype(f32)
+    flags = entry_flags(tail_ref[2 * width :].astype(i32))
+    masked = jnp.where(flags, both[:width], 0.0).astype(bf16)
+    kgr_ref[...] = raw_keys(masked, rot_ref)
+    vgr_ref[...] = jnp.transpose(both[width:].astype(bf16))
 
 
 def raw_kernel(groups, rot_ref, *refs):
@@ -513,7 +523,7 @@
         if step > 1:
             x = functools.reduce(jnp.add, [part.astype(f32) for part in parts])
             send = None if pack is None else pack(x)
-        masks = (step, 2 * step, 3 * step) if 2 * step < size else (step,)
+        masks = (3 * step, 2 * step, step) if 2 * step < size else (step,)
         swaps = [[(i, i ^ m) for i in range(size)] for m in masks]
         out = x if send is None else send
         parts = [x]
@@ -595,6 +605,9 @@
     )(*key_args)
     halo = lax.ppermute(halo, "seq", forward)
 
+    def in_hbm(args):
+        return [pltpu.with_memory_space_constraint(x, pltpu.HBM) for x in args]
+
     skip = WINDOW // STEP
     pay_rows = width // 2 + 16
     query_args = (sinks, query_elements, query_exponents.T, output_gradient, query_clip_words)
@@ -617,17 +630,18 @@
             pltpu.VMEM((count, width), bf16),
             pltpu.VMEM((groups, count, head), bf16),
             pltpu.VMEM((groups, count, head), bf16),
-            pltpu.VMEM((count, width), f32),
-            pltpu.VMEM((count, width), f32),
-            pltpu.VMEM((width // 2, LANES), f32),
+            pltpu.VMEM((width, count), f32),
+            pltpu.VMEM((width, count), f32),
+            pltpu.VMEM((width, head), f32),
             pltpu.VMEM((8, lanes), f32),
             pltpu.VMEM((8, lanes), f32),
         ]
 
-    params = pltpu.CompilerParams(vmem_limit_bytes=67043328)
+    params = pltpu.CompilerParams(vmem_limit_bytes=40 * 1024 * 1024)
     full_q = jax.ShapeDtypeStruct((rows, query_width), bf16)
     full_k = jax.ShapeDtypeStruct((rows, width), bf16)
-    edge_f = jax.ShapeDtypeStruct((WINDOW, 2 * width), f32)
+    edge_f = jax.ShapeDtypeStruct((2 * width, WINDOW), f32)
+    tail_f = jax.ShapeDtypeStruct((2 * width + words, WINDOW), f32)
     pay_f = jax.ShapeDtypeStruct((pay_rows, LANES), f32)
     grad_q, kgr, vgr, front, tail, part = pl.pallas_call(
         functools.partial(main_kernel, groups, per_group),
@@ -637,18 +651,18 @@
             pl.BlockSpec((STEP, query_width), lambda b: (b + skip, 0)),
             whole((rows, width)),
             whole((rows, width)),
-            whole((WINDOW, 2 * width)),
-            whole((WINDOW, 2 * width)),
+            whole((2 * width, WINDOW)),
+            whole((2 * width + words, WINDOW)),
             whole((pay_rows, LANES)),
         ],
-        out_shape=[full_q, full_k, full_k, edge_f, edge_f, pay_f],
+        out_shape=[full_q, full_k, full_k, edge_f, tail_f, pay_f],
         scratch_shapes=scratch(rows),
         compiler_params=params,
         cost_estimate=pl.CostEstimate(
             flops=60_000_000_000, bytes_accessed=60_000_000, transcendentals=0
         ),
         name="attend",
-    )(*query_args, *key_args, rot)
+    )(*in_hbm((*query_args, *key_args, rot)))
 
     anywhere = pl.BlockSpec(memory_space=pl.ANY)
     grad_q, kgr, vgr, back, pay, send = pl.pallas_call(
@@ -659,7 +673,7 @@
         + [
             whole(rot.shape),
             whole((WINDOW, 2 * width + LANES)),
-            whole((WINDOW, 2 * width)),
+            whole((2 * width, WINDOW)),
             whole((pay_rows, LANES)),
             anywhere,
             anywhere,
@@ -669,7 +683,7 @@
             pl.BlockSpec((STEP, query_width), lambda b: (b, 0)),
             whole((WINDOW, width)),
             whole((WINDOW, width)),
-            whole((WINDOW, 2 * width)),
+            whole((2 * width, WINDOW)),
             whole((pay_rows, LANES)),
             whole((pay_rows, LANES)),
         ],
@@ -677,7 +691,7 @@
             full_q,
             full_k,
             full_k,
-            jax.ShapeDtypeStruct((WINDOW, 2 * width), bf16),
+            jax.ShapeDtypeStruct((2 * width, WINDOW), bf16),
             pay_f,
             jax.ShapeDtypeStruct((pay_rows, LANES), bf16),
         ],
@@ -685,7 +699,15 @@
         scratch_shapes=scratch(2 * WINDOW),
         compiler_params=params,
         name="front",
-    )(*query_args, *key_args, rot, halo, front, part, grad_q, kgr, vgr)
+    )(
+        *in_hbm((*query_args, *key_args, rot)),
+        halo,
+        front,
+        part,
+        grad_q,
+        kgr,
+        vgr,
+    )
 
     pays = addends(pay, "seq", send, functools.partial(packed, width // 2))
     back = lax.ppermute(back, "seq", backward)
@@ -693,22 +715,21 @@
         keys_kernel,
         grid=(1,),
         in_specs=[
-            whole((WINDOW, 2 * width)),
-            whole((WINDOW, 2 * width)),
-            pl.BlockSpec((words, WINDOW), lambda b: (0, last)),
+            whole((2 * width + words, WINDOW)),
+            whole((2 * width, WINDOW)),
             whole(rot.shape),
             anywhere,
             anywhere,
         ],
         out_specs=[pl.BlockSpec((WINDOW, width), lambda b: (last, 0))] * 2,
         out_shape=[full_k, full_k],
-        input_output_aliases={4: 0, 5: 1},
+        input_output_aliases={3: 0, 4: 1},
         cost_estimate=pl.CostEstimate(
             flops=1_000_000_000, bytes_accessed=3_000_000, transcendentals=0
         ),
         compiler_params=pltpu.CompilerParams(vmem_limit_bytes=8 * 1024 * 1024),
         name="keys",
-    )(tail, back, key_words, rot, kgr, vgr)
+    )(tail, back, rot, kgr, vgr)
     raw, square, sink_sum = pl.pallas_call(
         functools.partial(raw_kernel, groups),
         out_shape=[
@@ -718,7 +739,7 @@
         ],
         compiler_params=pltpu.CompilerParams(vmem_limit_bytes=8 * 1024 * 1024),
         name="raw",
-    )(rotation, *pays)
+    )(rot, *pays)
     grad_rotation = pl.pallas_call(
         functools.partial(scale_kernel, limit_value),
         out_shape=jax.ShapeDtypeStruct((groups, head, head), f32),

time: 63.7 us -> 55 us (0.86)
  local copies, waits for them, and re-layouts: 3.6 us -> 0.01 us
  Pallas kernels: 34.2 us -> 31.6 us
  waiting for transfers between devices: 9.02 us -> 7.73 us
  other arithmetic: 1.01 us -> 0.12 us
    unnamed x8 -> x2, local copies, waits for them, and re-layouts: 3.6 us -> 0.01 us
    pallas_call x1, Pallas kernels: 24.1 us -> 22.2 us  [device_work(): pl.pallas_call(functools.partial(main_kernel, groups, per_group), grid=(r...]
    ppermute x7, waiting for transfers between devices: 9.01 us -> 7.73 us  [addends(): parts.append(lax.ppermute(out, axis, swap))]
    sub x1, other arithmetic: 0.91 us -> 0.03 us  [packed(): rest = x - lax.reduce_precision(x, 8, 7)]
    ppermute x1, starting transfers between devices: 5.53 us -> 4.86 us  [device_work(): halo = lax.ppermute(halo, 'seq', forward)]
  transfers between devices with their start and end apart: 9 -> 9, of which waited for: 5 -> 6; matrix products, arithmetic and copies ran while one was open for 2% -> 0% of each run, Pallas kernels for 41% -> 43%
where the time goes in v4:
time: 55 us; the launch traced here: 54.7 us
  Pallas kernels  31.6 us (57%)
  starting transfers between devices  14.6 us (27%)
  waiting for transfers between devices  7.73 us (14%)
  between operations  0.69 us (1%)
    pallas_call x1, Pallas kernels, device_work(): pl.pallas_call(functools.partial(main_kernel, groups, per_group), grid=(r...  22.2 us
    ppermute x7, starting transfers between devices, addends(): parts.append(lax.ppermute(out, axis, swap))  8.43 us
    ppermute x7, waiting for transfers between devices, addends(): parts.append(lax.ppermute(out, axis, swap))  7.73 us
    pallas_call x1, Pallas kernels, device_work(): pl.pallas_call(functools.partial(front_kernel, groups, per_group), grid=(...  5.15 us
    ppermute x1, starting transfers between devices, device_work(): halo = lax.ppermute(halo, 'seq', forward)  4.86 us
    pallas_call x1, Pallas kernels, device_work(): pl.pallas_call(halo_kernel, grid=(1,), in_specs=key_specs(WINDOW, last),...  1.83 us
    ppermute x1, starting transfers between devices, device_work(): back = lax.ppermute(back, 'seq', backward)  1.28 us
  transfers between devices with their start and end apart: 9, of which 6 were waited for; matrix products, arithmetic and copies ran while one was open for 0% of the time, Pallas kernels for 43%

profile of v4, /device:TPU:0, one launch (start us, length us, event | category | flops | bytes accessed | tf_op | source)
XLA Modules:
  0.0 54.7 jit_solution(5209196198520655641)
XLA Ops:
  0.6 1.8 %halo.1 = bf16[128,640]{1,0:T(8,128)(2,1)} custom-call(bf16[1024,256]{1,0:T(8,128)(2,1)} %k_ref.5, s32[8,1024]{1,0:T(8,128)} %bitcast.12, bf16[1024,256]{1,0:T(8,128)(2,1)} %v_ref.5, s32[8,1024]{1,0:T(8,128)} %bitcast.15, s32[16,1024]{1,0:T(8,128)} %bitcast.9), custom_call_target="tpu_custom_call" | custom-call | tf_op jit(solution)/shard_map/halo/pallas_call | solution.py:598
  2.5 4.9 %collective-permute-start = (bf16[128,640]{1,0:T(8,128)(2,1)}, bf16[128,640]{1,0:T(8,128)(2,1)S(1)}, u32[]{:S(2)}, u32[]{:S(2)}) collective-permute-start(bf16[128,640]{1,0:T(8,128)(2,1)} %halo.1), channel_id=1, source_target_pairs={{0,2},{2,4},{4,6},{6,8},{8,10},{10,12},{12,14},{14,16},{16,18},{18... | collective-permute-start | bytes 491528 | tf_op jit(solution)/shard_map/ppermute | solution.py:606
  7.3 22.2 %attend.1 = (bf16[1024,2048]{1,0:T(8,128)(2,1)}, bf16[1024,256]{1,0:T(8,128)(2,1)}, bf16[1024,256]{1,0:T(8,128)(2,1)}, f32[512,128]{1,0:T(8,128)S(1)}, f32[528,128]{1,0:T(8,128)S(1)}, /*index=5*/f32[144,128]{1,0:T(8,128)S(1)}) custom-call(f32[32]{0:T(128)} %sink_ref.3, bf16[1024,2048]{1,0:T(8,128)(2,1)} %q_ref.3, s32[64,1024]{1,0:T(8,128)} %bitcast.7, ...), custom_call_target="tpu_custom_call" | custom-call | flops 60000002048 | bytes 60000000 | tf_op jit(solution)/shard_map/attend/pallas_call | solution.py:646
  29.5 0.0 collective-permute-done.halo_ref
  29.5 0.0 copy-start
  29.5 5.1 %front.1 = (bf16[1024,2048]{1,0:T(8,128)(2,1)}, bf16[1024,256]{1,0:T(8,128)(2,1)}, bf16[1024,256]{1,0:T(8,128)(2,1)}, bf16[512,128]{1,0:T(8,128)(2,1)S(1)}, f32[...) custom-call(f32[32]{0:T(128)} %sink_ref.3, ...), custom_call_target="tpu_custom_call", output_to_operand_aliasing={{0}: (14, {}), {1}: (15, {}), {2}: (16, {})} | custom-call | tf_op jit(solution)/shard_map/front/pallas_call | solution.py:668
  34.7 2.4 %collective-permute-start.2 = (bf16[144,128]{1,0:T(8,128)(2,1)S(1)}, bf16[144,128]{1,0:T(8,128)(2,1)S(1)}, u32[]{:S(2)}, u32[]{:S(2)}) collective-permute-start(bf16[144,128]{1,0:T(8,128)(2,1)S(1)} %get-tuple-element.35), channel_id=1, source_target_pairs={{0,6},{2,4},{4,2},{6,0},{8,14},{10,12},{12,10},{14,8},{16,22},{18,... | collective-permute-start | bytes 110600 | tf_op jit(solution)/shard_map/ppermute | solution.py:531
  37.1 0.5 collective-permute-start.3
  37.6 0.5 collective-permute-start.4
  38.2 1.3 %collective-permute-start.1 = (bf16[512,128]{1,0:T(8,128)(2,1)S(1)}, bf16[512,128]{1,0:T(8,128)(2,1)S(1)}, u32[]{:S(2)}, u32[]{:S(2)}) collective-permute-start(bf16[512,128]{1,0:T(8,128)(2,1)S(1)} %get-tuple-element.29), channel_id=1, source_target_pairs={{2,0},{4,2},{6,4},{8,6},{10,8},{12,10},{14,12},{16,14},{18,16},{20... | collective-permute-start | bytes 393224 | tf_op jit(solution)/shard_map/ppermute | solution.py:713
  39.5 0.2 collective-permute-done.2
  39.6 1.4 %collective-permute-done.3 = bf16[144,128]{1,0:T(8,128)(2,1)S(1)} collective-permute-done((bf16[144,128]{1,0:T(8,128)(2,1)S(1)}, bf16[144,128]{1,0:T(8,128)(2,1)S(1)}, u32[]{:S(2)}, u32[]{:S(2)}) %collective-permute-start.3) | collective-permute-done | bytes 36896 | tf_op jit(solution)/shard_map/ppermute | solution.py:531
  41.1 0.7 %collective-permute-done.4 = bf16[144,128]{1,0:T(8,128)(2,1)S(1)} collective-permute-done((bf16[144,128]{1,0:T(8,128)(2,1)S(1)}, bf16[144,128]{1,0:T(8,128)(2,1)S(1)}, u32[]{:S(2)}, u32[]{:S(2)}) %collective-permute-start.4) | collective-permute-done | bytes 36896 | tf_op jit(solution)/shard_map/ppermute | solution.py:531
  41.9 0.1 fusion
  42.0 4.3 %collective-permute-start.5 = (bf16[144,128]{1,0:T(8,128)(2,1)S(1)}, bf16[144,128]{1,0:T(8,128)(2,1)S(1)}, u32[]{:S(2)}, u32[]{:S(2)}) collective-permute-start(bf16[144,128]{1,0:T(8,128)(2,1)S(1)} %fusion), channel_id=1, source_target_pairs={{0,24},{2,26},{4,28},{6,30},{8,16},{10,18},{12,20},{14,22},{16,8},... | collective-permute-start | bytes 110600 | tf_op jit(solution)/shard_map/ppermute | solution.py:531
  46.3 0.0 collective-permute-start.6
  46.3 0.6 %collective-permute-start.7 = (bf16[144,128]{1,0:T(8,128)(2,1)S(1)}, bf16[144,128]{1,0:T(8,128)(2,1)S(1)}, u32[]{:S(2)}, u32[]{:S(2)}) collective-permute-start(bf16[144,128]{1,0:T(8,128)(2,1)S(1)} %fusion), channel_id=1, source_target_pairs={{0,8},{2,10},{4,12},{6,14},{8,0},{10,2},{12,4},{14,6},{16,24},{18,... | collective-permute-start | bytes 110600 | tf_op jit(solution)/shard_map/ppermute | solution.py:531
  46.9 2.7 %collective-permute-done.5.refs_1_ = bf16[144,128]{1,0:T(8,128)(2,1)S(1)} collective-permute-done((bf16[144,128]{1,0:T(8,128)(2,1)S(1)}, bf16[144,128]{1,0:T(8,128)(2,1)S(1)}, u32[]{:S(2)}, u32[]{:S(2)}) %collective-permute-start.5) | collective-permute-done | bytes 36896 | tf_op jit(solution)/shard_map/ppermute | solution.py:531
  49.6 1.5 %collective-permute-done.6.refs_2_ = bf16[144,128]{1,0:T(8,128)(2,1)S(1)} collective-permute-done((bf16[144,128]{1,0:T(8,128)(2,1)S(1)}, bf16[144,128]{1,0:T(8,128)(2,1)S(1)}, u32[]{:S(2)}, u32[]{:S(2)}) %collective-permute-start.6) | collective-permute-done | bytes 36896 | tf_op jit(solution)/shard_map/ppermute | solution.py:531
  51.1 0.0 collective-permute-done.7.refs_3_
  51.1 0.0 copy-done
  51.1 0.8 %raw.1 = (f32[4,64,64]{2,1,0:T(8,128)S(1)}, f32[8,128]{1,0:T(8,128)S(1)}, f32[1,32]{1,0:T(1,128)}) custom-call(f32[4,64,64]{2,1,0:T(8,128)S(1)} %copy-done, f32[144,128]{1,0:T(8,128)S(1)} %get-tuple-element.40.refs_0_, bf16[144,128]{1,0:T(8,128)(2,1)S(1)} %collective-permute-done.5.refs_1_, bf16[144,128]{1,0:T(8,128)(2,1)S(1)} %collective-permute-done.6.refs_2_, ...), custom_call_target="tpu_custom_call" | custom-call | tf_op jit(solution)/shard_map/raw/pallas_call | solution.py:733
  52.0 0.0 collective-permute-start.8
  52.0 1.2 %collective-permute-done.8.refs_1_ = f32[8,128]{1,0:T(8,128)S(1)} collective-permute-done((f32[8,128]{1,0:T(8,128)S(1)}, f32[8,128]{1,0:T(8,128)S(1)}, u32[]{:S(2)}, u32[]{:S(2)}) %collective-permute-start.8) | collective-permute-done | bytes 4128 | tf_op jit(solution)/shard_map/ppermute | solution.py:531
  53.1 0.7 %scale.1 = f32[4,64,64]{2,1,0:T(8,128)} custom-call(f32[4,64,64]{2,1,0:T(8,128)S(1)} %get-tuple-element.36.raw_ref, f32[8,128]{1,0:T(8,128)S(1)} %get-tuple-element.37.refs_0_, f32[8,128]{1,0:T(8,128)S(1)} %collective-permute-done.8.refs_1_), custom_call_target="tpu_custom_call" | custom-call | tf_op jit(solution)/shard_map/scale/pallas_call | solution.py:743
  53.8 0.0 collective-permute-done.1.back_ref
  53.9 0.9 %keys.1 = (bf16[1024,256]{1,0:T(8,128)(2,1)}, bf16[1024,256]{1,0:T(8,128)(2,1)}) custom-call(f32[528,128]{1,0:T(8,128)S(1)} %get-tuple-element.28.tail_ref, bf16[512,128]{1,0:T(8,128)(2,1)S(1)} %collective-permute-done.1.back_ref, f32[4,64,64]{2,1,0:T(8,128)S(1)} %copy-done, ...), custom_call_target="tpu_custom_call", output_to_operand_aliasing={{0}: (3, {}), {1}: (4, {})} | custom-call | flops 1000000000 | bytes 3000000 | tf_op jit(solution)/shard_map/keys/pallas_call | solution.py:714
  (3 shorter events, 0.0 us)
Async XLA Ops:
  2.5 27.1 %collective-permute-start = (bf16[128,640]{1,0:T(8,128)(2,1)}, bf16[128,640]{1,0:T(8,128)(2,1)S(1)}, u32[]{:S(2)}, u32[]{:S(2)}) collective-permute-start(bf16[128,640]{1,0:T(8,128)(2,1)} %halo.1), channel_id=1, source_target_pairs={{0,2},{2,4},{4,6},{6,8},{8,10},{10,12},{12,14},{14,16},{16,18},{18... | collective-permute-start | bytes 491528 | tf_op jit(solution)/shard_map/ppermute | solution.py:606
  29.5 21.6 %copy-start = (f32[4,64,64]{2,1,0:T(8,128)S(1)}, f32[4,64,64]{2,1,0:T(8,128)}, u32[]{:S(2)}) copy-start(f32[4,64,64]{2,1,0:T(8,128)} %rot_ref.7) | copy-start | bytes 196612
  34.7 5.0 %collective-permute-start.2 = (bf16[144,128]{1,0:T(8,128)(2,1)S(1)}, bf16[144,128]{1,0:T(8,128)(2,1)S(1)}, u32[]{:S(2)}, u32[]{:S(2)}) collective-permute-start(bf16[144,128]{1,0:T(8,128)(2,1)S(1)} %get-tuple-element.35), channel_id=1, source_target_pairs={{0,6},{2,4},{4,2},{6,0},{8,14},{10,12},{12,10},{14,8},{16,22},{18,... | collective-permute-start | bytes 110600 | tf_op jit(solution)/shard_map/ppermute | solution.py:531
  37.1 4.0 %collective-permute-start.3 = (bf16[144,128]{1,0:T(8,128)(2,1)S(1)}, bf16[144,128]{1,0:T(8,128)(2,1)S(1)}, u32[]{:S(2)}, u32[]{:S(2)}) collective-permute-start(bf16[144,128]{1,0:T(8,128)(2,1)S(1)} %get-tuple-element.35), channel_id=1, source_target_pairs={{0,4},{2,6},{4,0},{6,2},{8,12},{10,14},{12,8},{14,10},{16,20},{18,... | collective-permute-start | bytes 110600 | tf_op jit(solution)/shard_map/ppermute | solution.py:531
  37.6 4.2 %collective-permute-start.4 = (bf16[144,128]{1,0:T(8,128)(2,1)S(1)}, bf16[144,128]{1,0:T(8,128)(2,1)S(1)}, u32[]{:S(2)}, u32[]{:S(2)}) collective-permute-start(bf16[144,128]{1,0:T(8,128)(2,1)S(1)} %get-tuple-element.35), channel_id=1, source_target_pairs={{0,2},{2,0},{4,6},{6,4},{8,10},{10,8},{12,14},{14,12},{16,18},{18,... | collective-permute-start | bytes 110600 | tf_op jit(solution)/shard_map/ppermute | solution.py:531
  38.2 15.7 %collective-permute-start.1 = (bf16[512,128]{1,0:T(8,128)(2,1)S(1)}, bf16[512,128]{1,0:T(8,128)(2,1)S(1)}, u32[]{:S(2)}, u32[]{:S(2)}) collective-permute-start(bf16[512,128]{1,0:T(8,128)(2,1)S(1)} %get-tuple-element.29), channel_id=1, source_target_pairs={{2,0},{4,2},{6,4},{8,6},{10,8},{12,10},{14,12},{16,14},{18,16},{20... | collective-permute-start | bytes 393224 | tf_op jit(solution)/shard_map/ppermute | solution.py:713
  42.0 7.6 %collective-permute-start.5 = (bf16[144,128]{1,0:T(8,128)(2,1)S(1)}, bf16[144,128]{1,0:T(8,128)(2,1)S(1)}, u32[]{:S(2)}, u32[]{:S(2)}) collective-permute-start(bf16[144,128]{1,0:T(8,128)(2,1)S(1)} %fusion), channel_id=1, source_target_pairs={{0,24},{2,26},{4,28},{6,30},{8,16},{10,18},{12,20},{14,22},{16,8},... | collective-permute-start | bytes 110600 | tf_op jit(solution)/shard_map/ppermute | solution.py:531
  46.3 4.9 %collective-permute-start.6 = (bf16[144,128]{1,0:T(8,128)(2,1)S(1)}, bf16[144,128]{1,0:T(8,128)(2,1)S(1)}, u32[]{:S(2)}, u32[]{:S(2)}) collective-permute-start(bf16[144,128]{1,0:T(8,128)(2,1)S(1)} %fusion), channel_id=1, source_target_pairs={{0,16},{2,18},{4,20},{6,22},{8,24},{10,26},{12,28},{14,30},{16,0},... | collective-permute-start | bytes 110600 | tf_op jit(solution)/shard_map/ppermute | solution.py:531
  46.3 4.9 %collective-permute-start.7 = (bf16[144,128]{1,0:T(8,128)(2,1)S(1)}, bf16[144,128]{1,0:T(8,128)(2,1)S(1)}, u32[]{:S(2)}, u32[]{:S(2)}) collective-permute-start(bf16[144,128]{1,0:T(8,128)(2,1)S(1)} %fusion), channel_id=1, source_target_pairs={{0,8},{2,10},{4,12},{6,14},{8,0},{10,2},{12,4},{14,6},{16,24},{18,... | collective-permute-start | bytes 110600 | tf_op jit(solution)/shard_map/ppermute | solution.py:531
  52.0 1.2 %collective-permute-start.8 = (f32[8,128]{1,0:T(8,128)S(1)}, f32[8,128]{1,0:T(8,128)S(1)}, u32[]{:S(2)}, u32[]{:S(2)}) collective-permute-start(f32[8,128]{1,0:T(8,128)S(1)} %get-tuple-element.37.refs_0_), channel_id=1, source_target_pairs={{0,1},{1,0},{2,3},{3,2},{4,5},{5,4},{6,7},{7,6},{8,9},{9,8},{10,11... | collective-permute-start | bytes 12296 | tf_op jit(solution)/shard_map/ppermute | solution.py:531
